TPU v7x, 32 devices: a whole 2x2x4 slice. The times are simulated.
32 devices in a mesh: dp: 2 (over x), context: 4 (over y, core), tensor: 4 (over z).
Axes of the slice: x: 2, y: 2, z: 4, core: 2. Of those that a mesh axis runs over, the one named last changes fastest.
Arguments:
- hidden_in: bfloat16 [16, 1024, 576], P('dp', ('context', 'tensor')), may hold values from -6 to 6
- attn_gain: bfloat16 [576], P('dp'), may hold values from 0.099609375 to 1.8984375
- query_weight: bfloat16 [576, 576], P('dp'), may hold values from -0.25 to 0.25
- key_weight: bfloat16 [576, 192], P('dp'), may hold values from -0.25 to 0.25
- value_weight: bfloat16 [576, 192], P('dp'), may hold values from -0.25 to 0.25
- output_weight: bfloat16 [576, 576], P('dp'), may hold values from -3 to 3
- ffn_gain: bfloat16 [576], P('dp'), may hold values from 0.099609375 to 1.8984375
- gate_weight: bfloat16 [576, 1536], P('dp', 'tensor'), may hold values from -0.25 to 0.25
- up_weight: bfloat16 [576, 1536], P('dp', 'tensor'), may hold values from -0.25 to 0.25
- down_weight: bfloat16 [1536, 576], P('tensor', 'dp'), may hold values from -0.15625 to 0.15625
- out_grad: bfloat16 [16, 1024, 576], P('dp', ('context', 'tensor')), may hold values from -6 to 6
Outputs:
- hidden_out: bfloat16 [16, 1024, 576], P('dp', ('context', 'tensor'))
- input_grad: float32 [16, 1024, 576], P('dp', ('context', 'tensor'))
- attn_gain_grad: float32 [576], P('dp')
- query_weight_grad: float32 [576, 576], P('dp')
- key_weight_grad: float32 [576, 192], P('dp')
- value_weight_grad: float32 [576, 192], P('dp')
- output_weight_grad: float32 [576, 576], P('dp')
- ffn_gain_grad: float32 [576], P('dp')
- gate_weight_grad: float32 [576, 1536], P('dp', 'tensor')
- up_weight_grad: float32 [576, 1536], P('dp', 'tensor')
- down_weight_grad: float32 [1536, 576], P('tensor', 'dp')
All inputs are finite; a program needn't handle non-finite values.
Results may differ from a plain program's by a relative error of at most 0.024.
Values may be sent and summed in bfloat16 or wider, within the bound.
No kernel may reach another device: no remote copies, remote signals or barrier semaphores. Data moves between devices by JAX's collectives and lax.ppermute only.
A program may use at most 128 MiB of HBM per device.

v0:
```python
import jax
import jax.numpy as jnp
from jax import lax
from jax.sharding import PartitionSpec as P

HEADS = 9
KV_HEADS = 3
HEAD_DIM = 64


EPS = 1e-05
ROPE_BASE = 100000.0


def rotary(places, half_dim):
    frequency = ROPE_BASE ** (-jnp.arange(half_dim).astype(jnp.float32) / half_dim)
    angles = places.astype(jnp.float32)[:, None] * frequency[None, :]
    return (jnp.cos(angles), jnp.sin(angles))


def rotate(tensor, cosine_table, sine_table):
    half_dim = tensor.shape[-1] // 2
    first_half = tensor[..., :half_dim]
    second_half = tensor[..., half_dim:]
    cosine_b = cosine_table[:, None, :]
    sine_b = sine_table[:, None, :]
    return jnp.concatenate(
        [
            first_half * cosine_b - second_half * sine_b,
            second_half * cosine_b + first_half * sine_b,
        ],
        axis=-1,
    )


def rotate_back(tensor, cosine_table, sine_table):
    half_dim = tensor.shape[-1] // 2
    first_half = tensor[..., :half_dim]
    second_half = tensor[..., half_dim:]
    cosine_b = cosine_table[:, None, :]
    sine_b = sine_table[:, None, :]
    return jnp.concatenate(
        [
            first_half * cosine_b + second_half * sine_b,
            second_half * cosine_b - first_half * sine_b,
        ],
        axis=-1,
    )


def times_transposed(left, right):
    return lax.dot_general(
        left, right, (((1,), (1,)), ((), ())), preferred_element_type=jnp.float32
    )


def transposed_times(left, right):
    return lax.dot_general(
        left, right, (((0,), (0,)), ((), ())), preferred_element_type=jnp.float32
    )


def norm_back(grad_normed, normed, inverse):
    return inverse * (grad_normed - normed * jnp.mean(grad_normed * normed, axis=-1, keepdims=True))


def body(
    hidden_in,
    attn_gain,
    query_weight,
    key_weight,
    value_weight,
    output_weight,
    ffn_gain,
    gate_weight,
    up_weight,
    down_weight,
    out_grad,
):
    seq_count, local_len, model_width = hidden_in.shape
    kv_width = KV_HEADS * HEAD_DIM
    repeat = HEADS // KV_HEADS
    scale = HEAD_DIM ** (-0.5)
    token_rows = seq_count * local_len
    gain_one, query_all, key_all, value_all, output_all = (
        lax.all_gather(attn_gain, "dp", axis=0, tiled=True),
        lax.all_gather(query_weight, "dp", axis=0, tiled=True),
        lax.all_gather(key_weight, "dp", axis=0, tiled=True),
        lax.all_gather(value_weight, "dp", axis=0, tiled=True),
        lax.all_gather(output_weight, "dp", axis=0, tiled=True),
    )
    gain_two, gate_all, up_all, down_all = (
        lax.all_gather(ffn_gain, "dp", axis=0, tiled=True),
        lax.all_gather(gate_weight, "dp", axis=0, tiled=True),
        lax.all_gather(up_weight, "dp", axis=0, tiled=True),
        lax.all_gather(down_weight, "dp", axis=1, tiled=True),
    )
    places = lax.axis_index(("context", "tensor")) * local_len + jnp.arange(
        local_len, dtype=jnp.int32
    )
    cosine_table, sine_table = rotary(places, HEAD_DIM // 2)
    rows_in = hidden_in.astype(jnp.float32)
    inverse_one = lax.rsqrt(jnp.mean(rows_in * rows_in, axis=-1, keepdims=True) + EPS)
    normed_one = rows_in * inverse_one
    normed_low = (normed_one * gain_one.astype(jnp.float32)).astype(jnp.bfloat16)
    flat_normed = normed_low.reshape(token_rows, model_width)
    queries = jnp.dot(flat_normed, query_all, preferred_element_type=jnp.float32).reshape(
        seq_count, local_len, HEADS, HEAD_DIM
    )
    key_rows = jnp.dot(flat_normed, key_all, preferred_element_type=jnp.float32).reshape(
        seq_count, local_len, KV_HEADS, HEAD_DIM
    )
    value_rows = jnp.dot(flat_normed, value_all, preferred_element_type=jnp.float32).reshape(
        seq_count, local_len, kv_width
    )
    queries_low = rotate(queries, cosine_table, sine_table).astype(jnp.bfloat16)
    keys_low = (
        rotate(key_rows, cosine_table, sine_table)
        .astype(jnp.bfloat16)
        .reshape(seq_count, local_len, kv_width)
    )
    kv_local = jnp.concatenate([keys_low, value_rows.astype(jnp.bfloat16)], axis=-1)
    kv_whole = lax.all_gather(kv_local, ("context", "tensor"), axis=1, tiled=True)
    seq_len = kv_whole.shape[1]
    query_groups = queries_low.reshape(seq_count, local_len, KV_HEADS, repeat, HEAD_DIM)

    def attend_one(operands):
        query_seq, kv_seq = operands
        key_seq = kv_seq[:, :kv_width].reshape(seq_len, KV_HEADS, HEAD_DIM)
        value_seq = kv_seq[:, kv_width:].reshape(seq_len, KV_HEADS, HEAD_DIM)
        scores = (
            jnp.einsum("qgre,kge->grqk", query_seq, key_seq, preferred_element_type=jnp.float32)
            * scale
        )
        allowed = jnp.arange(seq_len)[None, :] <= places[:, None]
        scores = jnp.where(allowed, scores, -1e30)
        row_max = jnp.max(scores, axis=-1, keepdims=True)
        weights = jnp.exp(scores - row_max)
        row_sum = jnp.sum(weights, axis=-1, keepdims=True)
        probability = (weights / row_sum).astype(jnp.bfloat16)
        attended_seq = jnp.einsum(
            "grqk,kge->qgre", probability, value_seq, preferred_element_type=jnp.float32
        )
        return (
            attended_seq.reshape(local_len, HEADS * HEAD_DIM),
            row_max[..., 0] + jnp.log(row_sum[..., 0]),
        )

    attended, log_sums = lax.map(attend_one, (query_groups, kv_whole))
    attended_low = attended.astype(jnp.bfloat16)
    attended_flat = attended_low.reshape(token_rows, HEADS * HEAD_DIM)
    middle = rows_in + jnp.dot(
        attended_flat, output_all, preferred_element_type=jnp.float32
    ).reshape(seq_count, local_len, model_width)
    inverse_two = lax.rsqrt(jnp.mean(middle * middle, axis=-1, keepdims=True) + EPS)
    normed_two = middle * inverse_two
    ffn_low = (normed_two * gain_two.astype(jnp.float32)).astype(jnp.bfloat16)
    ffn_rows = lax.all_gather(ffn_low, "tensor", axis=1, tiled=True)
    block_len = ffn_rows.shape[1]
    wide_rows = seq_count * block_len
    flat_rows = ffn_rows.reshape(wide_rows, model_width)
    gate_act = jnp.dot(flat_rows, gate_all, preferred_element_type=jnp.float32)
    up_act = jnp.dot(flat_rows, up_all, preferred_element_type=jnp.float32)
    sigmoid_gate = jax.nn.sigmoid(gate_act)
    silu_act = gate_act * sigmoid_gate
    hidden_low = (silu_act * up_act).astype(jnp.bfloat16)
    partial_out = jnp.dot(hidden_low, down_all, preferred_element_type=jnp.float32).reshape(
        seq_count, block_len, model_width
    )
    ffn_out = lax.psum_scatter(
        partial_out.astype(jnp.bfloat16), "tensor", scatter_dimension=1, tiled=True
    ).astype(jnp.float32)
    hidden_out = (middle + ffn_out).astype(jnp.bfloat16)
    grad_rows = lax.all_gather(out_grad, "tensor", axis=1, tiled=True).reshape(
        wide_rows, model_width
    )
    grad_hidden = times_transposed(grad_rows, down_all)
    down_grad = transposed_times(hidden_low, grad_rows)
    grad_up_low = (grad_hidden * silu_act).astype(jnp.bfloat16)
    grad_gate_low = (
        grad_hidden * up_act * (sigmoid_gate * (1.0 + gate_act * (1.0 - sigmoid_gate)))
    ).astype(jnp.bfloat16)
    gate_grad = transposed_times(flat_rows, grad_gate_low)
    up_grad = transposed_times(flat_rows, grad_up_low)
    grad_ffn_part = (
        times_transposed(grad_gate_low, gate_all) + times_transposed(grad_up_low, up_all)
    ).reshape(seq_count, block_len, model_width)
    grad_ffn_in = lax.psum_scatter(
        grad_ffn_part.astype(jnp.bfloat16), "tensor", scatter_dimension=1, tiled=True
    ).astype(jnp.float32)
    ffn_gain_term = jnp.sum(grad_ffn_in * normed_two, axis=(0, 1))
    grad_middle = out_grad.astype(jnp.float32) + norm_back(
        grad_ffn_in * gain_two.astype(jnp.float32), normed_two, inverse_two
    )
    grad_mid_low = grad_middle.astype(jnp.bfloat16).reshape(token_rows, model_width)
    out_proj_grad = transposed_times(attended_flat, grad_mid_low)
    grad_attended = (
        times_transposed(grad_mid_low, output_all)
        .astype(jnp.bfloat16)
        .reshape(seq_count, local_len, KV_HEADS, repeat, HEAD_DIM)
    )
    attended_groups = attended.reshape(seq_count, local_len, KV_HEADS, repeat, HEAD_DIM)
    row_delta = jnp.transpose(
        jnp.sum(grad_attended.astype(jnp.float32) * attended_groups, axis=-1), (0, 2, 3, 1)
    )
    piece = lax.all_gather(kv_local, ("context", "tensor"), axis=1, tiled=True)
    piece_len = piece.shape[1]
    key_piece = piece[..., :kv_width].reshape(seq_count, piece_len, KV_HEADS, HEAD_DIM)
    value_piece = piece[..., kv_width:].reshape(seq_count, piece_len, KV_HEADS, HEAD_DIM)
    scores = (
        jnp.einsum("sqgre,skge->sgrqk", query_groups, key_piece, preferred_element_type=jnp.float32)
        * scale
    )
    allowed = jnp.arange(piece_len)[None, :] <= places[:, None]
    probs_full = jnp.exp(jnp.where(allowed, scores - log_sums[..., None], -1e30))
    grad_probs = jnp.einsum(
        "sqgre,skge->sgrqk", grad_attended, value_piece, preferred_element_type=jnp.float32
    )
    grad_scores = (probs_full * (grad_probs - row_delta[..., None])).astype(jnp.bfloat16)
    key_piece, probs_full, grad_scores = (key_piece, probs_full, grad_scores)
    grad_query = (
        jnp.einsum("sgrqk,skge->sqgre", grad_scores, key_piece, preferred_element_type=jnp.float32)
        * scale
    )
    piece_len = piece.shape[1]
    grad_keys = (
        jnp.einsum(
            "sgrqk,sqgre->skge", grad_scores, query_groups, preferred_element_type=jnp.float32
        )
        * scale
    )
    grad_values = jnp.einsum(
        "sgrqk,sqgre->skge",
        probs_full.astype(jnp.bfloat16),
        grad_attended,
        preferred_element_type=jnp.float32,
    )
    grad_piece = jnp.concatenate(
        [
            grad_keys.reshape(seq_count, piece_len, kv_width),
            grad_values.reshape(seq_count, piece_len, kv_width),
        ],
        axis=-1,
    )
    grad_kv = grad_piece
    grad_query, grad_kv = (grad_query, grad_kv)
    grad_kv_own = lax.psum_scatter(
        grad_kv.astype(jnp.bfloat16), ("context", "tensor"), scatter_dimension=1, tiled=True
    ).astype(jnp.float32)
    grad_keys_low = (
        rotate_back(
            grad_kv_own[..., :kv_width].reshape(seq_count, local_len, KV_HEADS, HEAD_DIM),
            cosine_table,
            sine_table,
        )
        .astype(jnp.bfloat16)
        .reshape(token_rows, kv_width)
    )
    grad_values_low = grad_kv_own[..., kv_width:].astype(jnp.bfloat16).reshape(token_rows, kv_width)
    grad_query_low = (
        rotate_back(
            grad_query.reshape(seq_count, local_len, HEADS, HEAD_DIM), cosine_table, sine_table
        )
        .astype(jnp.bfloat16)
        .reshape(token_rows, HEADS * HEAD_DIM)
    )
    query_grad = transposed_times(flat_normed, grad_query_low)
    key_grad = transposed_times(flat_normed, grad_keys_low)
    value_grad = transposed_times(flat_normed, grad_values_low)
    grad_normed = (
        times_transposed(grad_query_low, query_all)
        + times_transposed(grad_keys_low, key_all)
        + times_transposed(grad_values_low, value_all)
    )
    grad_normed = grad_normed.reshape(seq_count, local_len, model_width)
    attn_gain_term = jnp.sum(grad_normed * normed_one, axis=(0, 1))
    input_grad = grad_middle + norm_back(
        grad_normed * gain_one.astype(jnp.float32), normed_one, inverse_one
    )
    shards = (
        lax.psum_scatter(
            attn_gain_term.astype(jnp.bfloat16), "dp", scatter_dimension=0, tiled=True
        ).astype(jnp.float32),
        lax.psum_scatter(
            ffn_gain_term.astype(jnp.bfloat16), "dp", scatter_dimension=0, tiled=True
        ).astype(jnp.float32),
        lax.psum_scatter(
            query_grad.astype(jnp.bfloat16), "dp", scatter_dimension=0, tiled=True
        ).astype(jnp.float32),
        lax.psum_scatter(
            key_grad.astype(jnp.bfloat16), "dp", scatter_dimension=0, tiled=True
        ).astype(jnp.float32),
        lax.psum_scatter(
            value_grad.astype(jnp.bfloat16), "dp", scatter_dimension=0, tiled=True
        ).astype(jnp.float32),
        lax.psum_scatter(
            out_proj_grad.astype(jnp.bfloat16), "dp", scatter_dimension=0, tiled=True
        ).astype(jnp.float32),
        lax.psum_scatter(
            gate_grad.astype(jnp.bfloat16), "dp", scatter_dimension=0, tiled=True
        ).astype(jnp.float32),
        lax.psum_scatter(
            up_grad.astype(jnp.bfloat16), "dp", scatter_dimension=0, tiled=True
        ).astype(jnp.float32),
        lax.psum_scatter(
            down_grad.astype(jnp.bfloat16), "dp", scatter_dimension=1, tiled=True
        ).astype(jnp.float32),
    )
    attn_sums = (
        lax.psum(shards[0].astype(jnp.bfloat16), ("context", "tensor")).astype(jnp.float32),
        lax.psum(shards[1].astype(jnp.bfloat16), ("context", "tensor")).astype(jnp.float32),
        lax.psum(shards[2].astype(jnp.bfloat16), ("context", "tensor")).astype(jnp.float32),
        lax.psum(shards[3].astype(jnp.bfloat16), ("context", "tensor")).astype(jnp.float32),
        lax.psum(shards[4].astype(jnp.bfloat16), ("context", "tensor")).astype(jnp.float32),
        lax.psum(shards[5].astype(jnp.bfloat16), ("context", "tensor")).astype(jnp.float32),
    )
    ffn_sums = (
        lax.psum(shards[6].astype(jnp.bfloat16), "context").astype(jnp.float32),
        lax.psum(shards[7].astype(jnp.bfloat16), "context").astype(jnp.float32),
        lax.psum(shards[8].astype(jnp.bfloat16), "context").astype(jnp.float32),
    )
    return (
        hidden_out,
        input_grad,
        attn_sums[0],
        attn_sums[2],
        attn_sums[3],
        attn_sums[4],
        attn_sums[5],
        attn_sums[1],
        ffn_sums[0],
        ffn_sums[1],
        ffn_sums[2],
    )


def solution(mesh):
    placed = (
        P("dp", ("context", "tensor"), None),
        P("dp"),
        P("dp", None),
        P("dp", None),
        P("dp", None),
        P("dp", None),
        P("dp"),
        P("dp", "tensor"),
        P("dp", "tensor"),
        P("tensor", "dp"),
        P("dp", ("context", "tensor"), None),
    )
    return jax.shard_map(
        body,
        mesh=mesh,
        in_specs=placed,
        out_specs=(
            P("dp", ("context", "tensor"), None),
            P("dp", ("context", "tensor"), None),
            P("dp"),
            P("dp", None),
            P("dp", None),
            P("dp", None),
            P("dp", None),
            P("dp"),
            P("dp", "tensor"),
            P("dp", "tensor"),
            P("tensor", "dp"),
        ),
        check_vma=False,
    )
```

profile of v0, /device:TPU:0, one launch (start us, length us, event | category | flops | bytes accessed | tf_op | source)
XLA Modules:
  0.0 730.7 jit_solution(6010033176116477348)
XLA Ops:
  11.0 5.8 all-reduce.8
  18.2 6.1 all_gather.38
  25.0 6.0 all_gather.39
  33.8 8.2 %all_gather.41 = bf16[576,576]{1,0:T(8,128)(2,1)S(1)} all-gather(bf16[288,576]{1,0:T(8,128)(2,1)S(1)} %copy-done.29), channel_id=1, replica_groups=mesh['dp'=2,'context'=4,'tensor'=4] {'dp'}, dimensions={0}, use_global_device_ids=true | all-gather | bytes 995328 | tf_op jit(solution)/shard_map/all_gather | solution.py:87
  45.8 2.0 pad_maximum_fusion.1
  47.8 8.3 %all_gather.42 = bf16[576,576]{1,0:T(8,128)(2,1)} all-gather(bf16[288,576]{1,0:T(8,128)(2,1)S(1)} %copy-done.30), channel_id=1, replica_groups=mesh['dp'=2,'context'=4,'tensor'=4] {'dp'}, dimensions={0}, use_global_device_ids=true | all-gather | bytes 995328 | tf_op jit(solution)/shard_map/all_gather | solution.py:90
  56.1 40.9 %all-gather.4.cloned.1.call-done = bf16[8,1024,384]{2,1,0:T(8,128)(2,1)} async-done(((bf16[8,64,384]{2,1,0:T(8,128)(2,1)}), bf16[8,1024,384]{2,1,0:T(8,128)(2,1)}) %all-gather.4.cloned.1.call-update) | async-done | bytes 6291472 | tf_op jit(solution)/shard_map/all_gather | solution.py:123
  97.0 41.1 %while.13 = (s32[]{:T(128)}, f32[8,64,576]{1,2,0:T(8,128)}, f32[8,3,3,64]{3,2,1,0:T(4,128)}, bf16[8,1024,384]{2,1,0:T(8,128)(2,1)}, bf16[8,64,3,3,64]{4,1,3,2,0:T(8,128)(2,1)S(1)}, /*index=5*/s32[]{:T(128)}, s32[]{:T(128)}) while((s32[]{:T(128)}, f32[8,64,576]{1,2,0:T(8,128)}, f32[8,3,3,64]{3,2,1,0:T(4,128)}, ...), condition=%wide.region_4.5_spmd.clone, body=%wide.region_1.4_spmd.clone.sunk | while | flops 158137856 | bytes 13605225 | solution.py:149
  138.2 3.2 multiply_reduce_fusion
  144.2 8.3 %all_gather.45 = bf16[576,384]{1,0:T(8,128)(2,1)} all-gather(bf16[288,384]{1,0:T(8,128)(2,1)S(1)} %copy-done.31), channel_id=1, replica_groups=mesh['dp'=2,'context'=4,'tensor'=4] {'dp'}, dimensions={0}, use_global_device_ids=true | all-gather | bytes 663552 | tf_op jit(solution)/shard_map/all_gather | solution.py:94
  152.6 7.5 %all_gather.46 = bf16[576,384]{1,0:T(8,128)(2,1)} all-gather(bf16[288,384]{1,0:T(8,128)(2,1)S(1)} %copy-done.32), channel_id=1, replica_groups=mesh['dp'=2,'context'=4,'tensor'=4] {'dp'}, dimensions={0}, use_global_device_ids=true | all-gather | bytes 663552 | tf_op jit(solution)/shard_map/all_gather | solution.py:95
  160.1 7.2 all_gather.47
  167.2 29.8 %all-gather.6.cloned.1.call-done = bf16[8,256,576]{2,1,0:T(8,128)(2,1)} async-done(((bf16[8,64,576]{2,1,0:T(8,128)(2,1)}), bf16[8,256,576]{2,1,0:T(8,128)(2,1)}) %all-gather.6.cloned.1.call-update) | async-done | bytes 2359312 | tf_op jit(solution)/shard_map/all_gather | solution.py:158
  197.0 3.6 fusion.65
  200.7 3.4 fusion.64
  204.1 48.1 %all-gather.8.cloned.1.call-done = bf16[8,256,576]{2,1,0:T(8,128)(2,1)} async-done(((bf16[8,64,576]{2,1,0:T(8,128)(2,1)}), bf16[8,256,576]{2,1,0:T(8,128)(2,1)}) %all-gather.8.cloned.1.call-update) | async-done | bytes 2359312 | tf_op jit(solution)/shard_map/all_gather | solution.py:174
  252.2 6.8 multiply_convert_fusion
  260.6 1.4 add_convert_fusion
  262.0 2.6 copy.73
  264.8 1.5 copy-done.38
  266.3 3.6 convolution_convert_fusion.3
  270.2 6.6 fusion.62
  276.8 6.3 copy.75
  283.1 5.0 copy.74
  288.1 4.4 convolution_convert_fusion.5
  292.5 9.3 %fusion.67 = f32[8,3,1024,64,3]{2,3,4,1,0:T(8,128)} fusion(bf16[8,1024,3,64,1]{1,3,4,2,0:T(8,128)(2,1)S(1)} %bitcast.200, bf16[8,64,3,3,64]{4,1,3,2,0:T(8,128)(2,1)} %copy-done.6), kind=kOutput, calls=%fused_computation.125 | convolution fusion | flops 603979776 | bytes 22609920 | tf_op jit(solution)/shard_map/sqgre,skge->sgrqk/dot_general | solution.py:211
  301.8 2.2 convolution_convert_fusion.4
  304.0 11.8 %reduce-scatter.13.cloned.1.call-done = bf16[8,64,576]{2,1,0:T(8,128)(2,1)} async-done(((bf16[8,256,576]{2,1,0:T(8,128)(2,1)}), bf16[8,64,576]{2,1,0:T(8,128)(2,1)}) %reduce-scatter.13.cloned.1.call-update) | async-done | bytes 589840 | tf_op jit(solution)/shard_map/reduce_scatter | solution.py:188
  315.8 2.2 fusion.37
  318.0 1.5 fusion.56
  320.4 1.5 convolution_convert_fusion.2
  321.9 2.7 reshape.243
  324.6 3.6 fusion.26
  328.2 10.1 %bitcast_convert_fusion = bf16[8,3,64,1024]{3,2,1,0:T(8,128)(2,1)} fusion(f32[8,3,1024,64,3]{2,3,4,1,0:T(8,128)} %fusion.67, f32[8,3,3,64]{3,2,1,0:T(4,128)S(1)} %copy-done.39, pred[64,1024]{1,0:T(8,128)(4,1)S(1)} %iota_compare_fusion.1, bf16[8,64,3,3,64]{1,0,4,3,2:T(8,128)(2,1)S(1)} %copy-done.18), kind=kOutput, calls=%fused_computation.31 | convolution fusion | flops 624427008 | bytes 22693888 | tf_op jit(solution)/shard_map/sgrqk,sqgre->skge/dot_general | solution.py:232
  338.3 6.2 copy.83
  344.4 11.8 %fusion.12 = bf16[8,3,3,64,1024]{4,3,2,1,0:T(8,128)(2,1)S(1)} fusion(f32[8,3,1024,64,3]{2,3,4,1,0:T(8,128)} %fusion.67, f32[8,3,3,64]{3,2,1,0:T(4,128)S(1)} %copy.78, f32[8,3,3,64]{3,2,1,0:T(4,128)S(1)} %copy-done.39, pred[64,1024]{1,0:T(8,128)(4,1)S(1)} %iota_compare_fusion.1, bf16[8,1024,3,64,1]{1,3,4,2,0:T(8,128)(2,1)} %bitcast.218, ...), kind=kOutput, calls=%fused_computation.20 | convolution fusion | flops 632291328 | bytes 32149504 | tf_op jit(solution)/shard_map/sqgre,skge->sgrqk/dot_general | solution.py:216
  356.3 4.1 fusion.22
  360.9 6.2 copy.82
  367.1 8.3 %pad_maximum_fusion = bf16[8,1024,384]{2,1,0:T(8,128)(2,1)} fusion(bf16[8,1024,192]{2,1,0:T(8,128)(2,1)} %copy.83, bf16[8,1024,192]{2,1,0:T(8,128)(2,1)} %copy.82), kind=kLoop, calls=%fused_computation.30 | loop fusion | flops 12582912 | bytes 12582912 | tf_op jit(solution)/shard_map/concatenate | solution.py:238
  376.5 3.4 bitcast_convert_fusion.1
  379.9 6.2 convolution_multiply_fusion
  388.3 1.6 convolution_convert_fusion.1
  390.0 70.2 %reduce-scatter.15.cloned.1.call-done = bf16[8,64,384]{2,1,0:T(8,128)(2,1)} async-done(((bf16[8,1024,384]{2,1,0:T(8,128)(2,1)}), bf16[8,64,384]{2,1,0:T(8,128)(2,1)}) %reduce-scatter.15.cloned.1.call-update) | async-done | bytes 393232 | tf_op jit(solution)/shard_map/reduce_scatter | solution.py:247
  460.2 2.0 slice_convert_fusion
  465.6 2.9 convolution_convert_fusion
  468.5 2.6 copy.72
  471.9 24.1 %all-reduce.14.cloned.1.call-done = (bf16[288,384]{1,0:T(8,128)(2,1)}, bf16[288,384]{1,0:T(8,128)(2,1)}, bf16[384,288]{0,1:T(8,128)(2,1)}) async-done(((bf16[288,384]{1,0:T(8,128)(2,1)}, bf16[288,384]{1,0:T(8,128)(2,1)}, bf16[384,288]{0,1:T(8,128)(2,1)}), (bf16[288,384]{1,0:T(8,128)(2,1)}, bf16[288,384]{1,0:T(8,128)(2,1)}, bf16[384,288]{0,1:T(8,128)(2,1)})) %all-reduce.14.cloned.1.call-update) | async-done | bytes 663568 | tf_op jit(solution)/shard_map/psum | solution.py:318
  496.1 1.7 convert_element_type.241
  497.8 1.7 convert_element_type.243
  499.5 1.8 convert_element_type.245
  504.6 1.7 copy.86
  506.8 8.8 %reduce-scatter.23.cloned.1.call-done = bf16[288,576]{1,0:T(8,128)(2,1)} async-done(((bf16[576,576]{1,0:T(8,128)(2,1)}), bf16[288,576]{1,0:T(8,128)(2,1)}) %reduce-scatter.23.cloned.1.call-update) | async-done | bytes 331792 | tf_op jit(solution)/shard_map/reduce_scatter | solution.py:296
  515.6 19.8 %reduce-scatter.17.cloned.1.call-done = bf16[288,576]{1,0:T(8,128)(2,1)} async-done(((bf16[576,576]{1,0:T(8,128)(2,1)}), bf16[288,576]{1,0:T(8,128)(2,1)}) %reduce-scatter.17.cloned.1.call-update) | async-done | bytes 331792 | tf_op jit(solution)/shard_map/reduce_scatter | solution.py:287
  535.4 14.2 %reduce-scatter.21.cloned.1.call-done = bf16[288,192]{1,0:T(8,128)(2,1)} async-done(((bf16[576,192]{1,0:T(8,128)(2,1)}), bf16[288,192]{1,0:T(8,128)(2,1)}) %reduce-scatter.21.cloned.1.call-update) | async-done | bytes 110608 | tf_op jit(solution)/shard_map/reduce_scatter | solution.py:293
  549.7 14.9 %reduce-scatter.19.cloned.1.call-done = bf16[288,192]{1,0:T(8,128)(2,1)} async-done(((bf16[576,192]{1,0:T(8,128)(2,1)}), bf16[288,192]{1,0:T(8,128)(2,1)}) %reduce-scatter.19.cloned.1.call-update) | async-done | bytes 110608 | tf_op jit(solution)/shard_map/reduce_scatter | solution.py:290
  564.6 4.9 all-reduce.7
  569.7 34.5 %all-reduce.4 = (bf16[288]{0:T(512)(128)(2,1)S(1)}, bf16[288]{0:T(512)(128)(2,1)S(1)}) all-reduce(bf16[288]{0:T(512)(128)(2,1)S(1)} %dynamic-slice.3, bf16[288]{0:T(512)(128)(2,1)S(1)} %dynamic-slice.5), channel_id=1, replica_groups=mesh['dp'=2,'context'=4,'tensor'=4] {'context','tensor'}, use_global_device_ids=true, to_apply=%region_14.15 | all-reduce | flops 576 | bytes 2304 | tf_op jit(solution)/shard_map/psum | solution.py:310
  605.4 14.5 %reduce-scatter.11.cloned.1.call-done = bf16[8,64,576]{2,1,0:T(8,128)(2,1)} async-done(((bf16[8,256,576]{2,1,0:T(8,128)(2,1)}), bf16[8,64,576]{2,1,0:T(8,128)(2,1)}) %reduce-scatter.11.cloned.1.call-update) | async-done | bytes 589840 | tf_op jit(solution)/shard_map/reduce_scatter | solution.py:170
  619.9 3.5 fusion.42
  623.4 93.3 %all-reduce.12.cloned.1.call-done = (bf16[288,576]{1,0:T(8,128)(2,1)}, bf16[288,192]{1,0:T(8,128)(2,1)}, bf16[288,192]{1,0:T(8,128)(2,1)}, bf16[288,576]{1,0:T(8,128)(2,1)}) async-done(((bf16[288,576]{1,0:T(8,128)(2,1)}, bf16[288,192]{1,0:T(8,128)(2,1)}, bf16[288,192]{1,0:T(8,128)(2,1)}, bf16[288,576]{1,0:T(8,128)(2,1)}), (bf16[288,576]{1,0:T(8,128)(2,1)}, bf16[288,192]{1,0:T(8,128)(2,1)}, ...) | async-done | bytes 884752 | tf_op jit(solution)/shard_map/psum | solution.py:312
  716.7 1.6 convert_element_type.233
  718.3 1.6 convert_element_type.235
  720.0 1.9 convert_element_type.231
  721.9 1.9 convert_element_type.237
  (246 shorter events, 70.7 us)
Async XLA Ops:
  7.2 23.8 %copy-start.8 = (bf16[8,64,576]{2,1,0:T(8,128)(2,1)S(1)}, bf16[8,64,576]{2,1,0:T(8,128)(2,1)}, u32[]{:S(2)}) copy-start(bf16[8,64,576]{2,1,0:T(8,128)(2,1)} %param.13) | copy-start | bytes 1769476
  7.2 89.8 %all-gather.4.cloned.1.call-start = ((), (), s32[]{:S(2)}) async-start(), calls=%async_computation.10 | async-start | bytes 6684672 | tf_op jit(solution)/shard_map/all_gather | solution.py:123
  16.9 14.8 %copy-start.34 = (f32[576]{0:T(1024)}, f32[576]{0:T(1024)S(1)}, u32[]{:S(2)}) copy-start(f32[576]{0:T(1024)S(1)} %convert_element_type.199) | copy-start | bytes 6916
  18.2 13.5 %copy-start.36 = (f32[8,64]{1,0:T(8,128)}, f32[8,64]{1,0:T(8,128)S(1)}, u32[]{:S(2)}) copy-start(f32[8,64]{1,0:T(8,128)S(1)} %add_rsqrt_fusion.1) | copy-start | bytes 6148
  24.3 0.7 copy-start.25
  31.0 0.7 copy-start.23
  31.2 11.1 %copy-start.10 = (bf16[8,64,576]{2,1,0:T(8,128)(2,1)}, bf16[8,64,576]{2,1,0:T(8,128)(2,1)S(1)}, u32[]{:S(2)}) copy-start(bf16[8,64,576]{2,1,0:T(8,128)(2,1)S(1)} %fusion.38) | copy-start | bytes 1769476
  32.2 1.6 copy-start.29
  33.7 163.3 %all-gather.6.cloned.1.call-start = ((), (), s32[]{:S(2)}) async-start(), calls=%async_computation.11 | async-start | bytes 3276800 | tf_op jit(solution)/shard_map/all_gather | solution.py:158
  42.0 1.5 copy-start.13
  45.8 2.0 copy-start.30
  138.1 3.2 copy-start.6
  141.3 1.1 copy-start.3
  141.3 2.9 copy-start.31
  141.4 11.2 %copy-start.32 = (bf16[288,384]{1,0:T(8,128)(2,1)S(1)}, bf16[288,384]{1,0:T(8,128)(2,1)}, u32[]{:S(2)}) copy-start(bf16[288,384]{1,0:T(8,128)(2,1)} %param.21) | copy-start | bytes 663556
  141.4 18.7 %copy-start.33 = (bf16[384,288]{0,1:T(8,128)(2,1)S(1)}, bf16[384,288]{0,1:T(8,128)(2,1)}, u32[]{:S(2)}) copy-start(bf16[384,288]{0,1:T(8,128)(2,1)} %param.22) | copy-start | bytes 663556
  143.4 108.7 %all-gather.8.cloned.1.call-start = ((), (), s32[]{:S(2)}) async-start(), calls=%async_computation.13 | async-start | bytes 3276800 | tf_op jit(solution)/shard_map/all_gather | solution.py:174
  144.2 171.6 %reduce-scatter.13.cloned.1.call-start = ((), (), s32[]{:S(2)}) async-start(), calls=%async_computation.14 | async-start | bytes 3276800 | tf_op jit(solution)/shard_map/reduce_scatter | solution.py:188
  197.0 3.6 copy-start.1
  197.0 3.6 copy-start.20
  252.2 6.8 copy-start.21
  259.0 1.4 copy-start.12
  259.0 1.6 copy-start.15
  259.0 1.6 copy-start.19
  264.6 1.7 copy-start.38
  264.6 110.9 %reduce-scatter.29.cloned.1.call-start = ((), (), s32[]{:S(2)}) async-start(), calls=%async_computation.22 | async-start | bytes 663552 | tf_op jit(solution)/shard_map/reduce_scatter | solution.py:305
  270.0 105.5 %reduce-scatter.25.cloned.1.call-start = ((), (), s32[]{:S(2)}) async-start(), calls=%async_computation.20 | async-start | bytes 663552 | tf_op jit(solution)/shard_map/reduce_scatter | solution.py:299
  292.5 83.1 %reduce-scatter.27.cloned.1.call-start = ((), (), s32[]{:S(2)}) async-start(), calls=%async_computation.21 | async-start | bytes 663552 | tf_op jit(solution)/shard_map/reduce_scatter | solution.py:302
  292.5 9.3 %copy-start.2 = (bf16[8,256,576]{2,1,0:T(8,128)(2,1)S(1)}, bf16[8,256,576]{2,1,0:T(8,128)(2,1)}, u32[]{:S(2)}) copy-start(bf16[8,256,576]{2,1,0:T(8,128)(2,1)} %all-gather.6.cloned.1.call-done) | copy-start | bytes 7077892
  292.5 9.3 %copy-start.16 = (bf16[2048,384]{1,0:T(8,128)(2,1)S(1)}, bf16[2048,384]{1,0:T(8,128)(2,1)}, u32[]{:S(2)}) copy-start(bf16[2048,384]{1,0:T(8,128)(2,1)} %copy-done.15) | copy-start | bytes 4718596
  304.0 156.2 %reduce-scatter.15.cloned.1.call-start = ((), (), s32[]{:S(2)}) async-start(), calls=%async_computation.15 | async-start | bytes 6684672 | tf_op jit(solution)/shard_map/reduce_scatter | solution.py:247
  315.8 2.2 copy-start.4
  315.8 2.2 copy-start.17
  315.8 4.6 copy-start.22
  319.6 0.8 copy-start.28
  321.9 6.3 copy-start.39
  324.6 3.7 copy-start.18
  344.4 11.9 %copy-start.7 = (bf16[8,64,3,3,64]{4,1,3,2,0:T(8,128)(2,1)S(1)}, bf16[8,64,3,3,64]{4,1,3,2,0:T(8,128)(2,1)}, u32[]{:S(2)}) copy-start(bf16[8,64,3,3,64]{4,1,3,2,0:T(8,128)(2,1)} %copy-done.6) | copy-start | bytes 1769476
  356.3 4.6 copy-start
  375.4 120.6 %all-reduce.14.cloned.1.call-start = ((), (), s32[]{:S(2)}) async-start(), calls=%async_computation.24 | async-start | bytes 1327104 | tf_op jit(solution)/shard_map/psum | solution.py:318
  376.2 139.4 %reduce-scatter.23.cloned.1.call-start = ((), (), s32[]{:S(2)}) async-start(), calls=%async_computation.19 | async-start | bytes 1105920 | tf_op jit(solution)/shard_map/reduce_scatter | solution.py:296
  379.9 155.6 %reduce-scatter.17.cloned.1.call-start = ((), (), s32[]{:S(2)}) async-start(), calls=%async_computation.16 | async-start | bytes 1105920 | tf_op jit(solution)/shard_map/reduce_scatter | solution.py:287
  386.8 1.5 copy-start.11
  389.9 159.7 %reduce-scatter.21.cloned.1.call-start = ((), (), s32[]{:S(2)}) async-start(), calls=%async_computation.18 | async-start | bytes 442368 | tf_op jit(solution)/shard_map/reduce_scatter | solution.py:293
  460.2 2.2 copy-start.27
  463.6 100.9 %reduce-scatter.19.cloned.1.call-start = ((), (), s32[]{:S(2)}) async-start(), calls=%async_computation.17 | async-start | bytes 442368 | tf_op jit(solution)/shard_map/reduce_scatter | solution.py:290
  465.6 154.3 %reduce-scatter.11.cloned.1.call-start = ((), (), s32[]{:S(2)}) async-start(), calls=%async_computation.12 | async-start | bytes 3276800 | tf_op jit(solution)/shard_map/reduce_scatter | solution.py:170
  471.1 30.2 %copy-start.14 = (bf16[576,576]{1,0:T(8,128)(2,1)S(1)}, bf16[576,576]{1,0:T(8,128)(2,1)}, u32[]{:S(2)}) copy-start(bf16[576,576]{1,0:T(8,128)(2,1)} %copy-done.13) | copy-start | bytes 1990660
  471.1 30.8 %copy-start.24 = (bf16[576,192]{1,0:T(8,128)(2,1)S(1)}, bf16[576,192]{1,0:T(8,128)(2,1)}, u32[]{:S(2)}) copy-start(bf16[576,192]{1,0:T(8,128)(2,1)} %copy-done.23) | copy-start | bytes 663556
  471.2 245.5 %all-reduce.12.cloned.1.call-start = ((), (), s32[]{:S(2)}) async-start(), calls=%async_computation.23 | async-start | bytes 2064384 | tf_op jit(solution)/shard_map/psum | solution.py:312
  499.5 3.7 copy-start.26
  503.2 3.1 copy-start.9
  503.2 3.1 copy-start.35
  503.2 3.1 copy-start.37
  506.3 113.6 %copy-start.5 = (f32[8,64,576]{2,1,0:T(8,128)S(1)}, f32[8,64,576]{2,1,0:T(8,128)}, u32[]{:S(2)}) copy-start(f32[8,64,576]{2,1,0:T(8,128)} %copy-done.3) | copy-start | bytes 3538948
Sparse Core Ops, SparseCore 0:
  33.8 63.1 all-gather.3
  143.6 53.4 all-gather.5
  198.6 53.5 all-gather.7
  264.7 51.0 reduce-scatter.12
  318.5 13.2 reduce-scatter.28
  334.5 13.7 reduce-scatter.24
  351.1 13.7 reduce-scatter.26
  375.5 84.6 reduce-scatter.14
  462.8 33.2 all-reduce.13
  498.2 17.3 reduce-scatter.22
  518.4 16.9 reduce-scatter.16
  537.5 12.1 reduce-scatter.20
  552.5 12.0 reduce-scatter.18
  566.7 53.1 reduce-scatter.10
  623.6 93.0 all-reduce.11
where the time goes:
time: 739 us; the launch traced here: 731 us
  waiting for transfers between devices  392 us (53%)
  matrix products  99.5 us (13%)
  blocking collectives  96.9 us (13%)
  local copies, waits for them, and re-layouts  71.3 us (10%)
  other arithmetic  53.2 us (7%)
  between operations  16.5 us (2%)
    psum x1, waiting for transfers between devices, body(): lax.psum(shards[2].astype(jnp.bfloat16), ('context', 'tensor'))  93.3 us
    reduce_scatter x1, waiting for transfers between devices, body(): lax.psum_scatter(grad_kv.astype(jnp.bfloat16), ('context', 'tensor'), sca...  70.2 us
    all_gather x1, waiting for transfers between devices, body(): lax.all_gather(out_grad, 'tensor', axis=1, tiled=True)  48.1 us
    all_gather x1, waiting for transfers between devices, body(): lax.all_gather(kv_local, ('context', 'tensor'), axis=1, tiled=True)  40.9 us
    psum x1, blocking collectives, body(): lax.psum(shards[0].astype(jnp.bfloat16), ('context', 'tensor'))  34.5 us
    all_gather x1, waiting for transfers between devices, body(): ffn_rows = lax.all_gather(ffn_low, 'tensor', axis=1, tiled=True)  29.8 us
    psum x1, waiting for transfers between devices, body(): lax.psum(shards[6].astype(jnp.bfloat16), 'context').astype(jnp.float32)  24.1 us
    reduce_scatter x1, waiting for transfers between devices, body(): lax.psum_scatter(query_grad.astype(jnp.bfloat16), 'dp', scatter_dimension...  19.8 us
  transfers between devices with their start and end apart: 15, of which 12 were waited for; matrix products, arithmetic and copies ran while one was open for 20% of the time, Pallas kernels for 0%

commit v1 on v0

v1 whole, which is shorter than its diff:
```python
import functools
import jax
import jax.numpy as jnp
from jax import lax
from jax.experimental import pallas as pl
from jax.experimental.pallas import tpu as pltpu
from jax.sharding import PartitionSpec as P

HEADS = 9
KV_HEADS = 3
HEAD_DIM = 64
REPEAT = HEADS // KV_HEADS
QW = HEADS * HEAD_DIM
KW = KV_HEADS * HEAD_DIM
QKW = QW + KW
QKVW = QW + 2 * KW

EPS = 1e-05
ROPE_BASE = 100000.0
F32 = jnp.float32
BF16 = jnp.bfloat16
NEG = -1e30
QB = 128


def nn(left, right):
    return lax.dot_general(left, right, (((1,), (0,)), ((), ())), preferred_element_type=F32)


def nt(left, right):
    return lax.dot_general(left, right, (((1,), (1,)), ((), ())), preferred_element_type=F32)


def tn(left, right):
    return lax.dot_general(left, right, (((0,), (0,)), ((), ())), preferred_element_type=F32)


def swap_halves(tensor):
    width = tensor.shape[-1]
    lane = lax.broadcasted_iota(jnp.int32, tensor.shape, 1)
    ahead = pltpu.roll(tensor, width - HEAD_DIM // 2, 1)
    behind = pltpu.roll(tensor, HEAD_DIM // 2, 1)
    return jnp.where(lane % HEAD_DIM < HEAD_DIM // 2, ahead, behind)


def norm_of(rows):
    inverse = lax.rsqrt(jnp.mean(rows * rows, axis=-1, keepdims=True) + EPS)
    return rows * inverse, inverse


def norm_back(grad_normed, normed, inverse):
    return inverse * (grad_normed - normed * jnp.mean(grad_normed * normed, axis=-1, keepdims=True))


def vmem_call(body, outs, scratch=(), n_smem=0, n_in=0):
    return pl.pallas_call(
        body,
        out_shape=outs,
        in_specs=[pl.BlockSpec(memory_space=pltpu.SMEM)] * n_smem
        + [pl.BlockSpec(memory_space=pltpu.VMEM)] * n_in,
        out_specs=[pl.BlockSpec(memory_space=pltpu.VMEM)] * len(outs),
        scratch_shapes=list(scratch),
    )


def project_body(x_ref, gain_ref, w_ref, cos_ref, sin_ref, q_ref, kv_ref):
    tiles = QKW // cos_ref.shape[1]
    for r in range(0, x_ref.shape[0], QB):
        rows = pl.ds(r, QB)
        normed, _ = norm_of(x_ref[rows, :].astype(F32))
        low = (normed * gain_ref[...]).astype(BF16)
        qkv = nn(low, w_ref[:, :QKVW])
        qk = qkv[:, :QKW]
        cos = jnp.concatenate([cos_ref[rows, :]] * tiles, axis=1)
        sin = jnp.concatenate([sin_ref[rows, :]] * tiles, axis=1)
        turned = (qk * cos + swap_halves(qk) * sin).astype(BF16)
        q_ref[rows, :] = turned[:, :QW]
        kv_ref[rows, :KW] = turned[:, QW:]
        kv_ref[rows, KW:] = qkv[:, QKW:].astype(BF16)


def masks(core):
    shape = (QB, REPEAT * QB)
    key = lax.broadcasted_iota(jnp.int32, shape, 0)
    query = lax.broadcasted_iota(jnp.int32, shape, 1) % QB
    own = key <= query
    other = (key // 32) < (query // 32) + core
    return own, other


def stack_heads(ref, rows, group):
    return jnp.concatenate(
        [
            ref[rows, (group * REPEAT + t) * HEAD_DIM : (group * REPEAT + t + 1) * HEAD_DIM]
            for t in range(REPEAT)
        ],
        axis=0,
    )


def spans(block):
    parts = []
    for side in range(2):
        if block > 0:
            parts.append((side, 0, block * QB, False))
        parts.append((side, block * QB, QB, True))
    return parts


def attend_body(core_ref, q_ref, own_ref, oth_ref, o_ref, l_ref):
    mask = masks(core_ref[0])
    kv_refs = (own_ref, oth_ref)
    for block in range(q_ref.shape[0] // QB):
        rows = pl.ds(block * QB, QB)
        for group in range(KV_HEADS):
            kc = slice(group * HEAD_DIM, (group + 1) * HEAD_DIM)
            vc = slice(KW + group * HEAD_DIM, KW + (group + 1) * HEAD_DIM)
            qs = stack_heads(q_ref, rows, group) * BF16(HEAD_DIM**-0.5)
            scores = []
            for side, start, size, diagonal in spans(block):
                s = nt(kv_refs[side][pl.ds(start, size), kc], qs)
                if diagonal:
                    s = jnp.where(mask[side], s, NEG)
                scores.append(s)
            top = functools.reduce(
                jnp.maximum, [jnp.max(s, axis=0, keepdims=True) for s in scores]
            )
            total = 0.0
            out = 0.0
            for (side, start, size, diagonal), s in zip(spans(block), scores):
                w = jnp.exp(s - top)
                total = total + jnp.sum(w, axis=0, keepdims=True)
                out = out + tn(kv_refs[side][pl.ds(start, size), vc], w.astype(BF16))
            out = (out / total).T
            for t in range(REPEAT):
                head = group * REPEAT + t
                o_ref[rows, head * HEAD_DIM : (head + 1) * HEAD_DIM] = out[
                    t * QB : (t + 1) * QB, :
                ]
            l_ref[block * KV_HEADS + group : block * KV_HEADS + group + 1, :] = top + jnp.log(
                total
            )


def attend_back_body(
    core_ref, q_ref, own_ref, oth_ref, do_ref, o_ref, l_ref, dq_ref, down_ref, doth_ref, acc_ref
):
    mask = masks(core_ref[0])
    kv_refs = (own_ref, oth_ref)
    grads = (down_ref, acc_ref)
    for block in range(q_ref.shape[0] // QB - 1, -1, -1):
        rows = pl.ds(block * QB, QB)
        first = block == q_ref.shape[0] // QB - 1
        for group in range(KV_HEADS):
            kc = slice(group * HEAD_DIM, (group + 1) * HEAD_DIM)
            vc = slice(KW + group * HEAD_DIM, KW + (group + 1) * HEAD_DIM)
            qs = stack_heads(q_ref, rows, group) * BF16(HEAD_DIM**-0.5)
            do = stack_heads(do_ref, rows, group)
            o = stack_heads(o_ref, rows, group)
            delta = jnp.sum((do.astype(F32) * o).T, axis=0, keepdims=True)
            log_sum = l_ref[block * KV_HEADS + group : block * KV_HEADS + group + 1, :]
            dq = 0.0
            for side, start, size, diagonal in spans(block):
                part = pl.ds(start, size)
                key = kv_refs[side][part, kc]
                p = jnp.exp(nt(key, qs) - log_sum)
                if diagonal:
                    p = jnp.where(mask[side], p, 0.0)
                dp = nt(kv_refs[side][part, vc], do)
                ds = (p * (dp - delta)).astype(BF16)
                dv = nn(p.astype(BF16), do)
                dk = nn(ds, qs)
                dq = dq + tn(key, ds)
                if first:
                    grads[side][part, kc] = dk
                    grads[side][part, vc] = dv
                else:
                    grads[side][part, kc] += dk
                    grads[side][part, vc] += dv
            dq = (dq * HEAD_DIM**-0.5).T
            for t in range(REPEAT):
                head = group * REPEAT + t
                dq_ref[rows, head * HEAD_DIM : (head + 1) * HEAD_DIM] = dq[
                    t * QB : (t + 1) * QB, :
                ]
    doth_ref[...] = acc_ref[...].astype(BF16)


def tail_body(
    x_ref,
    gain_ref,
    w_ref,
    cos_ref,
    sin_ref,
    dq_ref,
    dkv_ref,
    recv_ref,
    dmid_ref,
    dx_ref,
    dw_ref,
    dgain_ref,
    low_ref,
    dqkv_ref,
):
    tiles = QKW // cos_ref.shape[1]
    gain_sum = 0.0
    for r in range(0, x_ref.shape[0], QB):
        rows = pl.ds(r, QB)
        normed, inverse = norm_of(x_ref[rows, :].astype(F32))
        low_ref[rows, :] = (normed * gain_ref[...]).astype(BF16)
        dkv = dkv_ref[rows, :] + recv_ref[rows, :].astype(F32)
        dqk = jnp.concatenate([dq_ref[rows, :], dkv[:, :KW]], axis=1)
        cos = jnp.concatenate([cos_ref[rows, :]] * tiles, axis=1)
        sin = jnp.concatenate([sin_ref[rows, :]] * tiles, axis=1)
        dqkv_ref[rows, :QKW] = (dqk * cos - swap_halves(dqk) * sin).astype(BF16)
        dqkv_ref[rows, QKW:] = dkv[:, KW:].astype(BF16)
        da = nt(dqkv_ref[rows, :], w_ref[:, :QKVW])
        gain_sum = gain_sum + jnp.sum(da * normed, axis=0, keepdims=True)
        dx_ref[rows, :] = (
            dmid_ref[rows, :] + norm_back(da * gain_ref[...], normed, inverse)
        ).astype(BF16)
    dgain_ref[...] = jnp.broadcast_to(gain_sum, dgain_ref.shape)
    dw_ref[...] = tn(low_ref[...], dqkv_ref[...]).astype(BF16)


def xor_pairs(count, distance):
    return [(i, i ^ distance) for i in range(count)]


def solution(mesh):
    dp = mesh.shape["dp"]
    ctx = mesh.shape["context"]
    ten = mesh.shape["tensor"]
    chips = ctx // 2

    def swap(value, axis, distance):
        return lax.ppermute(value, axis, xor_pairs(mesh.shape[axis], distance))

    def add_low(left, right):
        return (left.astype(F32) + right.astype(F32)).astype(BF16)

    def pick(value, index, axis=0):
        return lax.dynamic_index_in_dim(value, index, axis, keepdims=False)

    def to_sequences(value, low_rows):
        width = value.shape[-1]
        pieces = value.reshape(chips, ten, 2, low_rows, width).transpose(0, 2, 1, 3, 4)
        moved = lax.all_to_all(
            pieces.reshape(ctx * ten, low_rows, width), ("context", "tensor"), 0, 0, tiled=True
        )
        return moved.reshape(ctx * ten * low_rows, width)

    def to_blocks(value, low_rows):
        width = value.shape[-1]
        moved = lax.all_to_all(
            value.reshape(ctx * ten, low_rows, width), ("context", "tensor"), 0, 0, tiled=True
        )
        moved = moved.reshape(chips, 2, ten, low_rows, width).transpose(0, 2, 1, 3, 4)
        return moved.reshape(chips * ten, 2 * low_rows, width)

    def place_by(pieces_own_first, flag):
        own, other = pieces_own_first
        return jnp.where(flag == 0, jnp.stack([own, other]), jnp.stack([other, own]))

    def gather_attention(pack, ids):
        rows = pack.shape[0]
        if dp == 2:
            half = pick(pack.reshape(2, rows // 2, -1), ids["core"])
            far = swap(half, "dp", 1)
            mine = place_by((half, far), ids["dp"])
        else:
            half = pick(pack.reshape(2, rows // 2, -1), ids["core"])
            mine = lax.all_gather(half, "dp", axis=0, tiled=False)
        theirs = swap(mine, "context", 1)
        both = place_by((mine, theirs), ids["core"])
        return both.transpose(1, 0, 2, 3).reshape(dp, rows, -1)

    def gather_ffn(pack, ids):
        rows, cols = pack.shape
        quarter = pick(pack.reshape(ctx, rows // ctx, cols), ids["context"])
        strip = jnp.concatenate(
            [quarter] + [swap(quarter, "tensor", d) for d in range(1, ten)], axis=1
        )
        if dp == 2:
            half = rows // ctx // 2
            from_x = swap(strip, "dp", 1)
            from_y = swap(strip, "context", 2)
            corner = jnp.concatenate(
                [swap(from_x[:half], "context", 2), swap(from_y[half:], "dp", 1)], axis=0
            )
            mine = jnp.stack([jnp.stack([strip, from_y]), jnp.stack([from_x, corner])])
        else:
            from_y = swap(strip, "context", 2)
            mine = jnp.stack([strip, from_y])
            mine = lax.all_gather(mine, "dp", axis=0, tiled=False)
        theirs = swap(mine, "context", 1)
        whole = jnp.zeros((dp, ctx, rows // ctx, ten * cols), BF16)
        for x in range(dp):
            x_at = (ids["dp"] ^ x) if dp == 2 else x
            for y in range(chips):
                for c, source in enumerate((mine, theirs)):
                    q_at = ids["context"] ^ (2 * y + c)
                    whole = lax.dynamic_update_slice(
                        whole, source[x, y][None, None], (x_at, q_at, 0, 0)
                    )
        return whole.reshape(dp, rows, ten * cols)

    def reduce_pack(grads, ids, relative):
        rows, width = grads.shape[1:]
        quarter = rows // ctx
        cols = width // ten
        view = grads.reshape(dp, chips, 2, quarter, width)
        mine = pick(view, ids["core"], 2)
        got = swap(pick(view, 1 - ids["core"], 2), "context", 1)
        mine = add_low(mine, got)
        y_own, y_far = ids["context"] // 2, 1 - ids["context"] // 2
        if dp == 2:
            half = quarter // 2
            x_own, x_far = ids["dp"], 1 - ids["dp"]
            near, far = pick(mine, x_own), pick(mine, x_far)
            upper = add_low(near[:, :half], swap(far[:, :half], "dp", 1))
            side, away = pick(mine, y_own, 1), pick(mine, y_far, 1)
            lower = add_low(side[:, half:], swap(away[:, half:], "context", 2))
            upper = add_low(pick(upper, y_own), swap(pick(upper, y_far), "context", 2))
            lower = add_low(pick(lower, x_own), swap(pick(lower, x_far), "dp", 1))
            strip = jnp.concatenate([upper, lower], axis=0)
        else:
            mine = lax.psum_scatter(mine, "dp", scatter_dimension=0, tiled=False)
            strip = add_low(pick(mine, y_own), swap(pick(mine, y_far), "context", 2))
        strip = strip.reshape(quarter, ten, cols).transpose(1, 0, 2)
        total = pick(strip, 0 if relative else ids["tensor"]).astype(F32)
        for d in range(1, ten):
            chunk = pick(strip, d if relative else ids["tensor"] ^ d)
            total = total + swap(chunk, "tensor", d).astype(F32)
        piece = total.astype(BF16)
        if not relative:
            spread = jnp.zeros((ten, quarter, cols), BF16)
            for d in range(ten):
                part = piece if d == 0 else swap(piece, "tensor", d)
                spread = lax.dynamic_update_slice(spread, part[None], (ids["tensor"] ^ d, 0, 0))
            piece = spread.transpose(1, 0, 2).reshape(quarter, width)
        pair = place_by((piece, swap(piece, "context", 2)), ids["context"] // 2)
        whole = place_by((pair, swap(pair, "context", 1)), ids["core"])
        return whole.transpose(1, 0, 2, 3).reshape(rows, -1).astype(F32)

    def body(
        hidden_in,
        attn_gain,
        query_weight,
        key_weight,
        value_weight,
        output_weight,
        ffn_gain,
        gate_weight,
        up_weight,
        down_weight,
        out_grad,
    ):
        seq_count, local_len, width = hidden_in.shape
        part = attn_gain.shape[0]
        low_rows = local_len // 2
        tokens = ctx * ten * low_rows
        ff_part = gate_weight.shape[1]
        ids = {
            "dp": lax.axis_index("dp"),
            "context": lax.axis_index("context"),
            "tensor": lax.axis_index("tensor"),
        }
        ids["core"] = ids["context"] % 2
        core = ids["core"].reshape(1).astype(jnp.int32)

        attn_rows = -(-(part + 1) // 64) * 64
        ffn_rows = -(-(3 * part) // 64) * 64
        attn_width = QKVW + width
        gains = jnp.concatenate([attn_gain, ffn_gain, jnp.zeros((attn_width - 2 * part,), BF16)])
        attn_pack = jnp.concatenate(
            [
                jnp.concatenate([query_weight, key_weight, value_weight, output_weight], axis=1),
                gains[None],
                jnp.zeros((attn_rows - part - 1, attn_width), BF16),
            ],
            axis=0,
        )
        ffn_pack = jnp.concatenate(
            [
                gate_weight,
                up_weight,
                down_weight.T,
                jnp.zeros((ffn_rows - 3 * part, ff_part), BF16),
            ],
            axis=0,
        )
        attn_all = gather_attention(attn_pack, ids)
        ffn_all = gather_ffn(ffn_pack, ids)
        w_attn = attn_all[:, :part].reshape(width, attn_width)
        gain_one = attn_all[:, part, :part].reshape(1, width).astype(F32)
        gain_two = attn_all[:, part, part : 2 * part].reshape(1, width).astype(F32)
        out_all = w_attn[:, QKVW:]
        gate_all = ffn_all[:, :part].reshape(width, ten * ff_part)
        up_all = ffn_all[:, part : 2 * part].reshape(width, ten * ff_part)
        down_all = ffn_all[:, 2 * part : 3 * part].reshape(width, ten * ff_part)

        row = jnp.arange(tokens, dtype=jnp.int32)
        places = 2 * low_rows * (row // low_rows) + low_rows * ids["core"] + row % low_rows
        lane = jnp.arange(2 * HEAD_DIM, dtype=jnp.int32)
        frequency = ROPE_BASE ** (
            -(lane % (HEAD_DIM // 2)).astype(F32) / (HEAD_DIM // 2)
        )
        angles = places.astype(F32)[:, None] * frequency[None, :]
        cos = jnp.cos(angles)
        sin = jnp.where(lane % HEAD_DIM < HEAD_DIM // 2, -1.0, 1.0)[None, :] * jnp.sin(angles)

        x = to_sequences(hidden_in, low_rows)
        dy = to_sequences(out_grad, low_rows)

        q, kv = vmem_call(
            project_body,
            [
                jax.ShapeDtypeStruct((tokens, QW), BF16),
                jax.ShapeDtypeStruct((tokens, 2 * KW), BF16),
            ],
            n_in=5,
        )(x, gain_one, w_attn, cos, sin)
        kv_far = swap(kv, "context", 1)
        blocks = tokens // QB
        attended, log_sums = vmem_call(
            attend_body,
            [
                jax.ShapeDtypeStruct((tokens, QW), F32),
                jax.ShapeDtypeStruct((blocks * KV_HEADS, REPEAT * QB), F32),
            ],
            n_smem=1,
            n_in=3,
        )(core, q, kv, kv_far)

        rows_in = x.astype(F32)
        attended_low = attended.astype(BF16)
        middle = rows_in + nn(attended_low, out_all)
        normed_two, inverse_two = norm_of(middle)
        c = (normed_two * gain_two).astype(BF16)
        gate_act = nn(c, gate_all)
        up_act = nn(c, up_all)
        sigmoid = jax.nn.sigmoid(gate_act)
        silu = gate_act * sigmoid
        hidden = (silu * up_act).astype(BF16)
        hidden_out = (middle + nt(hidden, down_all)).astype(BF16)
        grad_hidden = nn(dy, down_all)
        d_up = (grad_hidden * silu).astype(BF16)
        d_gate = (grad_hidden * up_act * (sigmoid * (1.0 + gate_act * (1.0 - sigmoid)))).astype(
            BF16
        )
        down_grad = tn(dy, hidden)
        gate_grad = tn(c, d_gate)
        up_grad = tn(c, d_up)
        dc = nt(d_gate, gate_all) + nt(d_up, up_all)
        ffn_gain_term = jnp.sum(dc * normed_two, axis=0)
        d_middle = dy.astype(F32) + norm_back(dc * gain_two, normed_two, inverse_two)
        d_mid_low = d_middle.astype(BF16)
        out_grad_w = tn(attended_low, d_mid_low)
        d_attended = nt(d_mid_low, out_all).astype(BF16)

        ffn_grads = jnp.concatenate(
            [
                gate_grad.astype(BF16).reshape(dp, part, -1),
                up_grad.astype(BF16).reshape(dp, part, -1),
                down_grad.astype(BF16).reshape(dp, part, -1),
                jnp.zeros((dp, ffn_rows - 3 * part, ten * ff_part), BF16),
            ],
            axis=1,
        )
        ffn_sum = reduce_pack(ffn_grads, ids, True)

        dq, dkv, dkv_far = vmem_call(
            attend_back_body,
            [
                jax.ShapeDtypeStruct((tokens, QW), F32),
                jax.ShapeDtypeStruct((tokens, 2 * KW), F32),
                jax.ShapeDtypeStruct((tokens, 2 * KW), BF16),
            ],
            scratch=[pltpu.VMEM((tokens, 2 * KW), F32)],
            n_smem=1,
            n_in=6,
        )(core, q, kv, kv_far, d_attended, attended, log_sums)
        dkv_back = swap(dkv_far, "context", 1)
        dx, qkv_grad, gain_term = vmem_call(
            tail_body,
            [
                jax.ShapeDtypeStruct((tokens, width), BF16),
                jax.ShapeDtypeStruct((width, QKVW), BF16),
                jax.ShapeDtypeStruct((8, width), F32),
            ],
            scratch=[
                pltpu.VMEM((tokens, width), BF16),
                pltpu.VMEM((tokens, QKVW), BF16),
            ],
            n_in=9,
        )(x, gain_one, w_attn, cos, sin, dq, dkv, dkv_back, d_middle)

        gain_rows = jnp.concatenate(
            [
                gain_term[0].astype(BF16).reshape(dp, 1, part),
                ffn_gain_term.astype(BF16).reshape(dp, 1, part),
                jnp.zeros((dp, 1, attn_width - 2 * part), BF16),
            ],
            axis=2,
        )
        attn_grads = jnp.concatenate(
            [
                jnp.concatenate([qkv_grad, out_grad_w.astype(BF16)], axis=1).reshape(
                    dp, part, attn_width
                ),
                gain_rows,
                jnp.zeros((dp, attn_rows - part - 1, attn_width), BF16),
            ],
            axis=1,
        )
        attn_sum = reduce_pack(attn_grads, ids, False)

        out_blocks = to_blocks(hidden_out, low_rows)
        in_blocks = to_blocks(dx, low_rows).astype(F32)
        return (
            out_blocks,
            in_blocks,
            attn_sum[part, :part],
            attn_sum[:part, :QW],
            attn_sum[:part, QW:QKW],
            attn_sum[:part, QKW:QKVW],
            attn_sum[:part, QKVW:],
            attn_sum[part, part : 2 * part],
            ffn_sum[:part],
            ffn_sum[part : 2 * part],
            ffn_sum[2 * part : 3 * part].T,
        )

    weight_rows = P("dp", None)
    tokens_spec = P("dp", ("context", "tensor"), None)
    return jax.shard_map(
        body,
        mesh=mesh,
        in_specs=(
            tokens_spec,
            P("dp"),
            weight_rows,
            weight_rows,
            weight_rows,
            weight_rows,
            P("dp"),
            P("dp", "tensor"),
            P("dp", "tensor"),
            P("tensor", "dp"),
            tokens_spec,
        ),
        out_specs=(
            tokens_spec,
            tokens_spec,
            P("dp"),
            weight_rows,
            weight_rows,
            weight_rows,
            weight_rows,
            P("dp"),
            P("dp", "tensor"),
            P("dp", "tensor"),
            P("tensor", "dp"),
        ),
        check_vma=False,
    )
```

time: 739 us -> 328 us (0.44)
  waiting for transfers between devices: 392 us -> 103 us
  blocking collectives: 96.9 us -> 0 us
  matrix products: 99.5 us -> 32.3 us
  starting transfers between devices: 1.04 us -> 63 us
  Pallas kernels: 0 us -> 35.4 us
  other arithmetic: 53.2 us -> 27.8 us
  between operations: 16.5 us -> 1.8 us
  local copies, waits for them, and re-layouts: 71.3 us -> 58.9 us
    reduce_scatter x10 -> x0, waiting for transfers between devices: 154 us -> none  [the longest x1 70.2 us: body(): lax.psum_scatter(grad_kv.astype(jnp.bfloat16), ('context', 'tensor'), sca...]
    all_gather x3 -> x0, waiting for transfers between devices: 119 us -> none  [the longest x1 48.1 us: body(): lax.all_gather(out_grad, 'tensor', axis=1, tiled=True)]
    psum x2 -> x0, waiting for transfers between devices: 117 us -> none  [the longest x1 93.3 us: body(): lax.psum(shards[2].astype(jnp.bfloat16), ('context', 'tensor'))]
    ppermute x0 -> x35, waiting for transfers between devices: none -> 92.9 us  [swap(): return lax.ppermute(value, axis, xor_pairs(mesh.shape[axis], distance))]
    dot_general x42 -> x12, matrix products: 99.5 us -> 32.3 us  [the longest x4 14.9 us: nn(): lax.dot_general(left, right, (((1,), (0,)), ((), ())), preferred_element_...]
    all_gather x7 -> x0, blocking collectives: 51.6 us -> none  [the longest x1 8.35 us: body(): lax.all_gather(gate_weight, 'dp', axis=0, tiled=True)]
    ppermute x0 -> x35, starting transfers between devices: none -> 42.9 us  [swap(): return lax.ppermute(value, axis, xor_pairs(mesh.shape[axis], distance))]
    pallas_call x0 -> x4, Pallas kernels: none -> 35.4 us  [the longest x1 15.1 us: body(): vmem_call(attend_back_body, [jax.ShapeDtypeStruct((tokens, QW), F32), jax...]
  transfers between devices with their start and end apart: 15 -> 39, of which waited for: 12 -> 19; matrix products, arithmetic and copies ran while one was open for 20% -> 28% of each run, Pallas kernels for 0% -> 6%
where the time goes in v1:
time: 328 us; the launch traced here: 322 us
  waiting for transfers between devices  103 us (31%)
  starting transfers between devices  63 us (19%)
  local copies, waits for them, and re-layouts  58.9 us (18%)
  Pallas kernels  35.4 us (11%)
  matrix products  32.3 us (10%)
  other arithmetic  27.8 us (8%)
    ppermute x35, waiting for transfers between devices, swap(): return lax.ppermute(value, axis, xor_pairs(mesh.shape[axis], distance))  92.9 us
    ppermute x35, starting transfers between devices, swap(): return lax.ppermute(value, axis, xor_pairs(mesh.shape[axis], distance))  42.9 us
    pallas_call x1, Pallas kernels, body(): vmem_call(attend_back_body, [jax.ShapeDtypeStruct((tokens, QW), F32), jax...  15.1 us
    dot_general x4, matrix products, nn(): lax.dot_general(left, right, (((1,), (0,)), ((), ())), preferred_element_...  14.9 us
    dynamic_update_slice x8, local copies, waits for them, and re-layouts, gather_ffn(): lax.dynamic_update_slice(whole, source[x, y][None, None], (x_at, q_at, 0,...  12.3 us
    all_to_all x2, starting transfers between devices, to_blocks(): lax.all_to_all(value.reshape(ctx * ten, low_rows, width), ('context', 'te...  12 us
    dot_general x4, matrix products, tn(): lax.dot_general(left, right, (((0,), (0,)), ((), ())), preferred_element_...  10.6 us
    all_to_all x2, waiting for transfers between devices, to_sequences(): lax.all_to_all(pieces.reshape(ctx * ten, low_rows, width), ('context', 't...  10.1 us
  transfers between devices with their start and end apart: 39, of which 19 were waited for; matrix products, arithmetic and copies ran while one was open for 28% of the time, Pallas kernels for 6%

profile of v1, /device:TPU:0, one launch (start us, length us, event | category | flops | bytes accessed | tf_op | source)
XLA Modules:
  0.0 322.3 jit_solution(17922482873115023476)
XLA Ops:
  2.3 5.1 %collective-permute-start.5 = (bf16[224,384]{1,0:T(8,128)(2,1)S(1)}, bf16[224,384]{1,0:T(8,128)(2,1)S(1)}, u32[]{:S(2)}, u32[]{:S(2)}) collective-permute-start(bf16[224,384]{1,0:T(8,128)(2,1)S(1)} %dynamic-slice_bitcast_fusion.10), channel_id=1, source_target_pairs={{0,3},{1,2},{2,1},{3,0},{4,7},{5,6},{6,5},{7,4},{8,11},{9,10},{10,... | collective-permute-start | bytes 516104 | tf_op jit(solution)/shard_map/ppermute | solution.py:237
  10.2 2.5 collective-permute-done.5
  12.7 9.3 %collective-permute-done.4 = bf16[224,384]{1,0:T(8,128)(2,1)S(1)} collective-permute-done((bf16[224,384]{1,0:T(8,128)(2,1)S(1)}, bf16[224,384]{1,0:T(8,128)(2,1)S(1)}, u32[]{:S(2)}, u32[]{:S(2)}) %collective-permute-start.4) | collective-permute-done | bytes 172064 | tf_op jit(solution)/shard_map/ppermute | solution.py:237
  27.5 11.9 %collective-permute-done.6 = bf16[224,1536]{1,0:T(8,128)(2,1)S(1)} collective-permute-done((bf16[224,1536]{1,0:T(8,128)(2,1)S(1)}, bf16[224,1536]{1,0:T(8,128)(2,1)S(1)}, u32[]{:S(2)}, u32[]{:S(2)}) %collective-permute-start.6) | collective-permute-done | bytes 688160 | tf_op jit(solution)/shard_map/ppermute | solution.py:237
  45.8 12.9 %collective-permute-done.9 = bf16[112,1536]{1,0:T(8,128)(2,1)} collective-permute-done((bf16[112,1536]{1,0:T(8,128)(2,1)}, bf16[112,1536]{1,0:T(8,128)(2,1)}, u32[]{:S(2)}, u32[]{:S(2)}) %collective-permute-start.9) | collective-permute-done | bytes 344096 | tf_op jit(solution)/shard_map/ppermute | solution.py:237
  60.0 1.9 pad_maximum_fusion
  64.4 3.7 %all-to-all-start = ((bf16[16,32,576]{2,1,0:T(8,128)(2,1)}), bf16[16,32,576]{2,1,0:T(8,128)(2,1)S(1)}, u32[]{:S(2)}, u32[]{:S(2)}) async-start(bf16[16,32,576]{2,1,0:T(8,128)(2,1)} %bitcast.212), calls=%async_computation | async-start | bytes 1310720 | tf_op jit(solution)/shard_map/all_to_all | solution.py:248
  68.2 2.0 copy.139
  70.2 1.8 fusion.16
  72.2 1.9 fusion.2
  76.3 10.1 %all-to-all-done = bf16[16,32,576]{2,1,0:T(8,128)(2,1)S(1)} async-done(((bf16[16,32,576]{2,1,0:T(8,128)(2,1)}), bf16[16,32,576]{2,1,0:T(8,128)(2,1)S(1)}, u32[]{:S(2)}, u32[]{:S(2)}) %all-to-all-start) | async-done | bytes 589856 | tf_op jit(solution)/shard_map/all_to_all | solution.py:248
  86.5 4.4 %all-to-all-start.2 = ((bf16[16,32,576]{2,1,0:T(8,128)(2,1)}), bf16[16,32,576]{2,1,0:T(8,128)(2,1)}, u32[]{:S(2)}, u32[]{:S(2)}) async-start(bf16[16,32,576]{2,1,0:T(8,128)(2,1)} %bitcast.33), calls=%async_computation.2 | async-start | bytes 1310720 | tf_op jit(solution)/shard_map/all_to_all | solution.py:248
  90.9 4.4 %shard_map.194 = (bf16[512,576]{1,0:T(8,128)(2,1)}, bf16[512,384]{1,0:T(8,128)(2,1)}) custom-call(bf16[512,576]{1,0:T(8,128)(2,1)} %bitcast.195, f32[1,576]{1,0:T(1,128)} %reshape.460.gain_ref, bf16[576,1536]{1,0:T(8,128)(2,1)} %bitcast.190, f32[512,128]{1,0:T(8,128)} %get-tuple-element.73.cos_ref, f32[512,128]{1,0:T(8,128)} %get-tuple-element.72.sin_ref), custom_call_target="tpu_custom_call" | custom-call | tf_op jit(solution)/shard_map/pallas_call | solution.py:416
  95.5 3.0 broadcast_in_dim.57
  100.3 9.3 %shard_map.195 = (f32[512,576]{1,0:T(8,128)}, f32[12,384]{1,0:T(8,128)}) custom-call(s32[1]{0:T(128)} %bitcast.4.core_ref, bf16[512,576]{1,0:T(8,128)(2,1)} %get-tuple-element.21.q_ref, bf16[512,384]{1,0:T(8,128)(2,1)} %get-tuple-element.22.own_ref, bf16[512,384]{1,0:T(8,128)(2,1)} %copy-done.16), custom_call_target="tpu_custom_call" | custom-call | tf_op jit(solution)/shard_map/pallas_call | solution.py:426
  109.6 2.4 multiply_reduce_fusion.2
  112.2 2.6 slice_dynamic-update-slice_fusion.6
  115.7 2.0 slice_dynamic-update-slice_fusion.4
  118.6 2.0 slice_dynamic-update-slice_fusion.2
  121.5 2.0 slice_dynamic-update-slice_fusion
  123.6 4.3 %fusion.41 = (bf16[2,288,1536]{2,1,0:T(8,128)(2,1)}, bf16[2,288,1536]{2,1,0:T(8,128)(2,1)S(1)}, bf16[2,288,1536]{2,1,0:T(8,128)(2,1)S(1)}) fusion(bf16[2,896,1536]{2,1,0:T(8,128)(2,1)} %bitcast.23), kind=kLoop, calls=%fused_computation.152 | loop fusion | bytes 10616832 | tf_op jit(solution)/shard_map/slice | solution.py:401
  127.9 3.0 fusion.45
  130.9 3.0 fusion.46
  134.0 6.5 %multiply_convert_fusion = (bf16[512,1536]{1,0:T(8,128)(2,1)S(1)}, bf16[512,1536]{1,0:T(8,128)(2,1)S(1)}, bf16[512,1536]{1,0:T(8,128)(2,1)S(1)}) fusion(f32[512,1536]{1,0:T(8,128)} %fusion.45, f32[512,1536]{1,0:T(8,128)} %fusion.46, bf16[512,576]{1,0:T(8,128)(2,1)} %bitcast.34, bf16[576,1536]{1,0:T(8,128)(2,1)} %bitcast.223), kind=kOutput, calls=%fused_computation.4 | convolution fusion | flops 917766144 | bytes 13369344 | tf_op jit(solution)/shard_map/dot_general | solution.py:27
  140.5 2.3 fusion.4
  142.7 3.6 %convolution_convert_fusion = bf16[1536,576]{0,1:T(8,128)(2,1)} fusion(bf16[512,1536]{1,0:T(8,128)(2,1)S(1)} %get-tuple-element.39, bf16[512,576]{1,0:T(8,128)(2,1)} %bitcast.34), kind=kOutput, calls=%fused_computation.9 | convolution fusion | flops 906854400 | bytes 3932160 | tf_op jit(solution)/shard_map/dot_general | solution.py:35
  147.8 2.3 convolution_convert_fusion.1
  150.1 1.6 multiply_reduce_fusion
  154.8 2.1 copy.143.do_ref
  156.9 15.1 %shard_map.196 = (f32[512,576]{1,0:T(8,128)}, f32[512,384]{1,0:T(8,128)}, bf16[512,384]{1,0:T(8,128)(2,1)}) custom-call(s32[1]{0:T(128)} %bitcast.4.core_ref, bf16[512,576]{1,0:T(8,128)(2,1)} %get-tuple-element.21.q_ref, bf16[512,384]{1,0:T(8,128)(2,1)} %get-tuple-element.22.own_ref, bf16[512,384]{1,0:T(8,128)(2,1)} %copy-done.16, ...), custom_call_target="tpu_custom_call" | custom-call | tf_op jit(solution)/shard_map/pallas_call | solution.py:473
  172.9 5.9 %all-to-all-start.1 = ((bf16[16,32,576]{2,1,0:T(8,128)(2,1)}), bf16[16,32,576]{2,1,0:T(8,128)(2,1)}, u32[]{:S(2)}, u32[]{:S(2)}) async-start(bf16[16,32,576]{2,1,0:T(8,128)(2,1)} %bitcast.240), calls=%async_computation.1 | async-start | bytes 1310720 | tf_op jit(solution)/shard_map/all_to_all | solution.py:255
  178.9 4.0 %convolution_convert_fusion.2 = bf16[576,1536]{1,0:T(8,128)(2,1)} fusion(bf16[512,576]{1,0:T(8,128)(2,1)} %copy-done.22, bf16[512,1536]{1,0:T(8,128)(2,1)} %copy-done.28), kind=kOutput, calls=%fused_computation.11 | convolution fusion | flops 906854400 | bytes 3932160 | tf_op jit(solution)/shard_map/dot_general | solution.py:35
  182.9 6.7 %shard_map.197 = (bf16[512,576]{1,0:T(8,128)(2,1)}, bf16[576,960]{1,0:T(8,128)(2,1)}, f32[8,576]{1,0:T(8,128)}) custom-call(bf16[512,576]{1,0:T(8,128)(2,1)} %bitcast.197, f32[1,576]{1,0:T(1,128)} %reshape.460.gain_ref, bf16[576,1536]{1,0:T(8,128)(2,1)} %bitcast.191, f32[512,128]{1,0:T(8,128)} %get-tuple-element.73.cos_ref, ...), custom_call_target="tpu_custom_call" | custom-call | tf_op jit(solution)/shard_map/pallas_call | solution.py:485
  190.4 1.7 pad_maximum_fusion.1
  196.8 1.8 copy.189
  199.3 1.7 collective-permute-start.15
  202.6 4.9 %collective-permute-done.15 = bf16[2,40,1536]{2,1,0:T(8,128)(2,1)S(1)} collective-permute-done((bf16[2,40,1536]{2,1,0:T(8,128)(2,1)S(1)}, bf16[2,40,1536]{2,1,0:T(8,128)(2,1)S(1)}, u32[]{:S(2)}, u32[]{:S(2)}) %collective-permute-start.15) | collective-permute-done | bytes 245792 | tf_op jit(solution)/shard_map/ppermute | solution.py:237
  210.6 1.7 collective-permute-start.14
  212.6 6.0 %all-to-all-start.3 = ((bf16[16,32,576]{2,1,0:T(8,128)(2,1)}), bf16[16,32,576]{2,1,0:T(8,128)(2,1)S(1)}, u32[]{:S(2)}, u32[]{:S(2)}) async-start(bf16[16,32,576]{2,1,0:T(8,128)(2,1)} %bitcast.239), calls=%async_computation.3 | async-start | bytes 1310720 | tf_op jit(solution)/shard_map/all_to_all | solution.py:255
  220.3 1.7 reshape.453
  222.0 1.8 constant_dynamic-slice_fusion.4
  223.9 3.9 %collective-permute-start.19 = (bf16[80,384]{1,0:T(8,128)(2,1)S(1)}, bf16[80,384]{1,0:T(8,128)(2,1)S(1)}, u32[]{:S(2)}, u32[]{:S(2)}) collective-permute-start(bf16[80,384]{1,0:T(8,128)(2,1)S(1)} %bitcast.249), channel_id=1, source_target_pairs={{0,3},{1,2},{2,1},{3,0},{4,7},{5,6},{6,5},{7,4},{8,11},{9,10},{10,... | collective-permute-start | bytes 184328 | tf_op jit(solution)/shard_map/ppermute | solution.py:237
  228.5 7.4 %collective-permute-done.19 = bf16[80,384]{1,0:T(8,128)(2,1)S(1)} collective-permute-done((bf16[80,384]{1,0:T(8,128)(2,1)S(1)}, bf16[80,384]{1,0:T(8,128)(2,1)S(1)}, u32[]{:S(2)}, u32[]{:S(2)}) %collective-permute-start.19) | collective-permute-done | bytes 61472 | tf_op jit(solution)/shard_map/ppermute | solution.py:237
  236.0 5.9 %collective-permute-done.18 = bf16[80,384]{1,0:T(8,128)(2,1)S(1)} collective-permute-done((bf16[80,384]{1,0:T(8,128)(2,1)S(1)}, bf16[80,384]{1,0:T(8,128)(2,1)S(1)}, u32[]{:S(2)}, u32[]{:S(2)}) %collective-permute-start.18) | collective-permute-done | bytes 61472 | tf_op jit(solution)/shard_map/ppermute | solution.py:237
  242.0 1.9 collective-permute-start.21
  243.9 2.5 collective-permute-start.22
  246.4 2.0 copy.138
  249.8 1.8 dynamic_update_slice.44
  253.6 1.8 dynamic_update_slice.45
  255.4 1.8 dynamic_update_slice.46
  257.3 1.8 dynamic_update_slice.47
  260.9 2.5 fusion
  264.3 2.9 collective-permute-done.23
  270.0 10.8 %collective-permute-done.28 = bf16[2,112,1536]{2,1,0:T(8,128)(2,1)S(1)} collective-permute-done((bf16[2,112,1536]{2,1,0:T(8,128)(2,1)S(1)}, bf16[2,112,1536]{2,1,0:T(8,128)(2,1)S(1)}, u32[]{:S(2)}, u32[]{:S(2)}) %collective-permute-start.28) | collective-permute-done | bytes 688160 | tf_op jit(solution)/shard_map/ppermute | solution.py:237
  282.5 4.3 %collective-permute-done.26 = bf16[2,112,1536]{2,1,0:T(8,128)(2,1)S(1)} collective-permute-done((bf16[2,112,1536]{2,1,0:T(8,128)(2,1)S(1)}, bf16[2,112,1536]{2,1,0:T(8,128)(2,1)S(1)}, u32[]{:S(2)}, u32[]{:S(2)}) %collective-permute-start.26) | collective-permute-done | bytes 688160 | tf_op jit(solution)/shard_map/ppermute | solution.py:237
  287.0 2.4 collective-permute-start.27
  289.4 4.3 %collective-permute-done.29 = bf16[112,1536]{1,0:T(8,128)(2,1)S(1)} collective-permute-done((bf16[112,1536]{1,0:T(8,128)(2,1)S(1)}, bf16[112,1536]{1,0:T(8,128)(2,1)S(1)}, u32[]{:S(2)}, u32[]{:S(2)}) %collective-permute-start.29) | collective-permute-done | bytes 344096 | tf_op jit(solution)/shard_map/ppermute | solution.py:237
  293.8 3.1 collective-permute-done.27
  298.2 1.7 collective-permute-start.32
  300.0 2.8 collective-permute-start.30
  304.3 3.0 collective-permute-done.32
  307.3 6.1 %collective-permute-done.31 = bf16[224,384]{1,0:T(8,128)(2,1)S(1)} collective-permute-done((bf16[224,384]{1,0:T(8,128)(2,1)S(1)}, bf16[224,384]{1,0:T(8,128)(2,1)S(1)}, u32[]{:S(2)}, u32[]{:S(2)}) %collective-permute-start.31) | collective-permute-done | bytes 172064 | tf_op jit(solution)/shard_map/ppermute | solution.py:237
  313.5 1.8 collective-permute-start.33
  317.3 1.7 collective-permute-done.33
  (211 shorter events, 65.2 us)
Async XLA Ops:
  0.6 9.0 %copy-start.24 = (bf16[288,576]{1,0:T(8,128)(2,1)S(1)}, bf16[288,576]{1,0:T(8,128)(2,1)}, u32[]{:S(2)}) copy-start(bf16[288,576]{1,0:T(8,128)(2,1)} %param.13) | copy-start | bytes 995332
  0.7 9.0 %copy-start.26 = (bf16[288,192]{1,0:T(8,128)(2,1)S(1)}, bf16[288,192]{1,0:T(8,128)(2,1)}, u32[]{:S(2)}) copy-start(bf16[288,192]{1,0:T(8,128)(2,1)} %param.14) | copy-start | bytes 331780
  0.7 9.0 %copy-start.27 = (bf16[288,192]{1,0:T(8,128)(2,1)S(1)}, bf16[288,192]{1,0:T(8,128)(2,1)}, u32[]{:S(2)}) copy-start(bf16[288,192]{1,0:T(8,128)(2,1)} %param.15) | copy-start | bytes 331780
  0.7 9.0 %copy-start.25 = (bf16[288,576]{1,0:T(8,128)(2,1)S(1)}, bf16[288,576]{1,0:T(8,128)(2,1)}, u32[]{:S(2)}) copy-start(bf16[288,576]{1,0:T(8,128)(2,1)} %param.16) | copy-start | bytes 995332
  2.3 10.5 %collective-permute-start.5 = (bf16[224,384]{1,0:T(8,128)(2,1)S(1)}, bf16[224,384]{1,0:T(8,128)(2,1)S(1)}, u32[]{:S(2)}, u32[]{:S(2)}) collective-permute-start(bf16[224,384]{1,0:T(8,128)(2,1)S(1)} %dynamic-slice_bitcast_fusion.10), channel_id=1, source_target_pairs={{0,3},{1,2},{2,1},{3,0},{4,7},{5,6},{6,5},{7,4},{8,11},{9,10},{10,... | collective-permute-start | bytes 516104 | tf_op jit(solution)/shard_map/ppermute | solution.py:237
  7.4 14.6 %collective-permute-start.4 = (bf16[224,384]{1,0:T(8,128)(2,1)S(1)}, bf16[224,384]{1,0:T(8,128)(2,1)S(1)}, u32[]{:S(2)}, u32[]{:S(2)}) collective-permute-start(bf16[224,384]{1,0:T(8,128)(2,1)S(1)} %dynamic-slice_bitcast_fusion.10), channel_id=1, source_target_pairs={{0,2},{1,3},{2,0},{3,1},{4,6},{5,7},{6,4},{7,5},{8,10},{9,11},{10,... | collective-permute-start | bytes 516104 | tf_op jit(solution)/shard_map/ppermute | solution.py:237
  7.4 14.6 %collective-permute-start.3 = (bf16[224,384]{1,0:T(8,128)(2,1)S(1)}, bf16[224,384]{1,0:T(8,128)(2,1)S(1)}, u32[]{:S(2)}, u32[]{:S(2)}) collective-permute-start(bf16[224,384]{1,0:T(8,128)(2,1)S(1)} %dynamic-slice_bitcast_fusion.10), channel_id=1, source_target_pairs={{0,1},{1,0},{2,3},{3,2},{4,5},{5,4},{6,7},{7,6},{8,9},{9,8},{10,11... | collective-permute-start | bytes 516104 | tf_op jit(solution)/shard_map/ppermute | solution.py:237
  22.9 16.5 %collective-permute-start.6 = (bf16[224,1536]{1,0:T(8,128)(2,1)S(1)}, bf16[224,1536]{1,0:T(8,128)(2,1)S(1)}, u32[]{:S(2)}, u32[]{:S(2)}) collective-permute-start(bf16[224,1536]{1,0:T(8,128)(2,1)S(1)} %get-tuple-element.67), channel_id=1, source_target_pairs={{0,8},{4,12},{8,0},{12,4},{1,9},{5,13},{9,1},{13,5},{2,10},{6,14},... | collective-permute-start | bytes 2064392 | tf_op jit(solution)/shard_map/ppermute | solution.py:237
  24.5 18.3 %collective-permute-start.7 = (bf16[224,1536]{1,0:T(8,128)(2,1)S(1)}, bf16[224,1536]{1,0:T(8,128)(2,1)S(1)}, u32[]{:S(2)}, u32[]{:S(2)}) collective-permute-start(bf16[224,1536]{1,0:T(8,128)(2,1)S(1)} %get-tuple-element.67), channel_id=1, source_target_pairs={{0,16},{16,0},{1,17},{17,1},{2,18},{18,2},{3,19},{19,3},{4,20},{20... | collective-permute-start | bytes 2064392 | tf_op jit(solution)/shard_map/ppermute | solution.py:237
  27.0 34.9 %collective-permute-start = (bf16[160,1536]{1,0:T(8,128)(2,1)}, bf16[160,1536]{1,0:T(8,128)(2,1)S(1)}, u32[]{:S(2)}, u32[]{:S(2)}) collective-permute-start(bf16[160,1536]{1,0:T(8,128)(2,1)} %fusion.67), channel_id=1, source_target_pairs={{0,16},{16,0},{1,17},{17,1},{2,18},{18,2},{3,19},{19,3},{4,20},{20... | collective-permute-start | bytes 1474568 | tf_op jit(solution)/shard_map/ppermute | solution.py:237
  39.4 4.8 %copy-start.19 = (bf16[224,1536]{1,0:T(8,128)(2,1)}, bf16[224,1536]{1,0:T(8,128)(2,1)S(1)}, u32[]{:S(2)}) copy-start(bf16[224,1536]{1,0:T(8,128)(2,1)S(1)} %collective-permute-done.6) | copy-start | bytes 2064388
  40.3 18.4 %collective-permute-start.9 = (bf16[112,1536]{1,0:T(8,128)(2,1)}, bf16[112,1536]{1,0:T(8,128)(2,1)}, u32[]{:S(2)}, u32[]{:S(2)}) collective-permute-start(bf16[112,1536]{1,0:T(8,128)(2,1)} %slice.163), channel_id=1, source_target_pairs={{0,16},{16,0},{1,17},{17,1},{2,18},{18,2},{3,19},{19,3},{4,20},{20... | collective-permute-start | bytes 1032200 | tf_op jit(solution)/shard_map/ppermute | solution.py:237
  43.7 15.0 %collective-permute-start.8 = (bf16[112,1536]{1,0:T(8,128)(2,1)}, bf16[112,1536]{1,0:T(8,128)(2,1)}, u32[]{:S(2)}, u32[]{:S(2)}) collective-permute-start(bf16[112,1536]{1,0:T(8,128)(2,1)} %slice.162), channel_id=1, source_target_pairs={{0,8},{4,12},{8,0},{12,4},{1,9},{5,13},{9,1},{13,5},{2,10},{6,14},... | collective-permute-start | bytes 1032200 | tf_op jit(solution)/shard_map/ppermute | solution.py:237
  44.3 15.5 %copy-start.18 = (bf16[224,1536]{1,0:T(8,128)(2,1)S(1)}, bf16[224,1536]{1,0:T(8,128)(2,1)}, u32[]{:S(2)}) copy-start(bf16[224,1536]{1,0:T(8,128)(2,1)} %copy-done.17) | copy-start | bytes 2064388
  60.0 1.9 copy-start.2
  61.9 1.6 copy-start.21
  61.9 50.3 %collective-permute-start.10 = (bf16[2,2,224,1536]{3,2,1,0:T(8,128)(2,1)}, bf16[2,2,224,1536]{3,2,1,0:T(8,128)(2,1)}, u32[]{:S(2)}, u32[]{:S(2)}) collective-permute-start(bf16[2,2,224,1536]{3,2,1,0:T(8,128)(2,1)} %pad_maximum_fusion), channel_id=1, source_target_pairs={{0,4},{4,0},{8,12},{12,8},{1,5},{5,1},{9,13},{13,9},{2,6},{6,2},{1... | collective-permute-start | bytes 8257544 | tf_op jit(solution)/shard_map/ppermute | solution.py:237
  63.0 9.2 %collective-permute-start.1 = (bf16[2,160,1536]{2,1,0:T(8,128)(2,1)}, bf16[2,160,1536]{2,1,0:T(8,128)(2,1)}, u32[]{:S(2)}, u32[]{:S(2)}) collective-permute-start(bf16[2,160,1536]{2,1,0:T(8,128)(2,1)} %maximum_select_fusion.2), channel_id=1, source_target_pairs={{0,4},{4,0},{8,12},{12,8},{1,5},{5,1},{9,13},{13,9},{2,6},{6,2},{1... | collective-permute-start | bytes 2949128 | tf_op jit(solution)/shard_map/ppermute | solution.py:237
  64.4 22.0 %all-to-all-start = ((bf16[16,32,576]{2,1,0:T(8,128)(2,1)}), bf16[16,32,576]{2,1,0:T(8,128)(2,1)S(1)}, u32[]{:S(2)}, u32[]{:S(2)}) async-start(bf16[16,32,576]{2,1,0:T(8,128)(2,1)} %bitcast.212), calls=%async_computation | async-start | bytes 1310720 | tf_op jit(solution)/shard_map/all_to_all | solution.py:248
  86.5 4.5 %copy-start.7 = (bf16[16,32,576]{2,1,0:T(8,128)(2,1)}, bf16[16,32,576]{2,1,0:T(8,128)(2,1)S(1)}, u32[]{:S(2)}) copy-start(bf16[16,32,576]{2,1,0:T(8,128)(2,1)S(1)} %all-to-all-done) | copy-start | bytes 1769476
  86.5 47.5 %all-to-all-start.2 = ((bf16[16,32,576]{2,1,0:T(8,128)(2,1)}), bf16[16,32,576]{2,1,0:T(8,128)(2,1)}, u32[]{:S(2)}, u32[]{:S(2)}) async-start(bf16[16,32,576]{2,1,0:T(8,128)(2,1)} %bitcast.33), calls=%async_computation.2 | async-start | bytes 1310720 | tf_op jit(solution)/shard_map/all_to_all | solution.py:248
  95.3 4.2 %collective-permute-start.2 = (bf16[512,384]{1,0:T(8,128)(2,1)}, bf16[512,384]{1,0:T(8,128)(2,1)S(1)}, u32[]{:S(2)}, u32[]{:S(2)}) collective-permute-start(bf16[512,384]{1,0:T(8,128)(2,1)} %get-tuple-element.22.own_ref), channel_id=1, source_target_pairs={{0,4},{4,0},{8,12},{12,8},{1,5},{5,1},{9,13},{13,9},{2,6},{6,2},{1... | collective-permute-start | bytes 1179656 | tf_op jit(solution)/shard_map/ppermute | solution.py:237
  98.5 11.1 %copy-start = (bf16[2,288,1536]{2,1,0:T(8,128)(2,1)S(1)}, bf16[2,288,1536]{2,1,0:T(8,128)(2,1)}, u32[]{:S(2)}) copy-start(bf16[2,288,1536]{2,1,0:T(8,128)(2,1)} %slice.158) | copy-start | bytes 5308420
  112.0 3.7 %copy-start.5 = (f32[512,576]{1,0:T(8,128)}, f32[512,576]{1,0:T(8,128)S(1)}, u32[]{:S(2)}) copy-start(f32[512,576]{1,0:T(8,128)S(1)} %get-tuple-element.75) | copy-start | bytes 3538948
  112.2 18.7 %copy-start.22 = (bf16[512,576]{1,0:T(8,128)(2,1)}, bf16[512,576]{1,0:T(8,128)(2,1)S(1)}, u32[]{:S(2)}) copy-start(bf16[512,576]{1,0:T(8,128)(2,1)S(1)} %multiply_convert_fusion.3) | copy-start | bytes 1769476
  112.2 5.5 %copy-start.3 = (bf16[1,2,224,1536]{3,2,1,0:T(8,128)(2,1)S(1)}, bf16[1,2,224,1536]{3,2,1,0:T(8,128)(2,1)}, u32[]{:S(2)}) copy-start(bf16[1,2,224,1536]{3,2,1,0:T(8,128)(2,1)} %copy-done.2) | copy-start | bytes 4128772
  127.9 3.0 copy-start.13
  127.9 3.0 copy-start.11
  134.0 6.5 %copy-start.6 = (f32[512,576]{1,0:T(8,128)S(1)}, f32[512,576]{1,0:T(8,128)}, u32[]{:S(2)}) copy-start(f32[512,576]{1,0:T(8,128)} %copy-done.5) | copy-start | bytes 3538948
  134.0 6.5 %copy-start.15 = (bf16[2,288,1536]{2,1,0:T(8,128)(2,1)S(1)}, bf16[2,288,1536]{2,1,0:T(8,128)(2,1)}, u32[]{:S(2)}) copy-start(bf16[2,288,1536]{2,1,0:T(8,128)(2,1)} %get-tuple-element.42) | copy-start | bytes 5308420
  140.4 5.9 %copy-start.28 = (bf16[512,1536]{1,0:T(8,128)(2,1)}, bf16[512,1536]{1,0:T(8,128)(2,1)S(1)}, u32[]{:S(2)}) copy-start(bf16[512,1536]{1,0:T(8,128)(2,1)S(1)} %get-tuple-element.38) | copy-start | bytes 4718596
  142.7 3.6 %copy-start.14 = (bf16[2,288,1536]{2,1,0:T(8,128)(2,1)S(1)}, bf16[2,288,1536]{2,1,0:T(8,128)(2,1)}, u32[]{:S(2)}) copy-start(bf16[2,288,1536]{2,1,0:T(8,128)(2,1)} %copy-done.13) | copy-start | bytes 5308420
  147.8 2.4 copy-start.12
  153.3 19.0 %copy-start.1 = (f32[512,576]{1,0:T(8,128)}, f32[512,576]{1,0:T(8,128)S(1)}, u32[]{:S(2)}) copy-start(f32[512,576]{1,0:T(8,128)S(1)} %multiply_add_fusion.dmid_ref) | copy-start | bytes 3538948
  156.9 15.3 %copy-start.4 = (f32[512,576]{1,0:T(8,128)S(1)}, f32[512,576]{1,0:T(8,128)}, u32[]{:S(2)}) copy-start(f32[512,576]{1,0:T(8,128)} %get-tuple-element.23.o_ref) | copy-start | bytes 3538948
  172.0 10.9 %collective-permute-start.11 = (bf16[512,384]{1,0:T(8,128)(2,1)}, bf16[512,384]{1,0:T(8,128)(2,1)}, u32[]{:S(2)}, u32[]{:S(2)}) collective-permute-start(bf16[512,384]{1,0:T(8,128)(2,1)} %get-tuple-element.27), channel_id=1, source_target_pairs={{0,4},{4,0},{8,12},{12,8},{1,5},{5,1},{9,13},{13,9},{2,6},{6,2},{1... | collective-permute-start | bytes 1179656 | tf_op jit(solution)/shard_map/ppermute | solution.py:237
  172.9 39.7 %all-to-all-start.1 = ((bf16[16,32,576]{2,1,0:T(8,128)(2,1)}), bf16[16,32,576]{2,1,0:T(8,128)(2,1)}, u32[]{:S(2)}, u32[]{:S(2)}) async-start(bf16[16,32,576]{2,1,0:T(8,128)(2,1)} %bitcast.240), calls=%async_computation.1 | async-start | bytes 1310720 | tf_op jit(solution)/shard_map/all_to_all | solution.py:255
  192.7 1.5 copy-start.9
  192.8 2.0 copy-start.10
  192.9 2.4 copy-start.8
  193.0 5.9 %collective-permute-start.12 = (bf16[2,2,80,1536]{3,2,0,1:T(8,128)(2,1)S(1)}, bf16[2,2,80,1536]{3,2,0,1:T(8,128)(2,1)S(1)}, u32[]{:S(2)}, u32[]{:S(2)}) collective-permute-start(bf16[2,2,80,1536]{3,2,0,1:T(8,128)(2,1)S(1)} %bitcast.231), channel_id=1, source_target_pairs={{0,4},{4,0},{8,12},{12,8},{1,5},{5,1},{9,13},{13,9},{2,6},{6,2},{1... | collective-permute-start | bytes 2949128 | tf_op jit(solution)/shard_map/ppermute | solution.py:237
  198.6 62.3 %collective-permute-start.25 = (bf16[2,2,224,1536]{3,2,0,1:T(8,128)(2,1)}, bf16[2,2,224,1536]{3,2,0,1:T(8,128)(2,1)}, u32[]{:S(2)}, u32[]{:S(2)}) collective-permute-start(bf16[2,2,224,1536]{3,2,0,1:T(8,128)(2,1)} %bitcast.182), channel_id=1, source_target_pairs={{0,4},{4,0},{8,12},{12,8},{1,5},{5,1},{9,13},{13,9},{2,6},{6,2},{1... | collective-permute-start | bytes 8257544 | tf_op jit(solution)/shard_map/ppermute | solution.py:237
  199.3 8.2 %collective-permute-start.15 = (bf16[2,40,1536]{2,1,0:T(8,128)(2,1)S(1)}, bf16[2,40,1536]{2,1,0:T(8,128)(2,1)S(1)}, u32[]{:S(2)}, u32[]{:S(2)}) collective-permute-start(bf16[2,40,1536]{2,1,0:T(8,128)(2,1)S(1)} %slice.178), channel_id=1, source_target_pairs={{0,8},{4,12},{8,0},{12,4},{1,9},{5,13},{9,1},{13,5},{2,10},{6,14},... | collective-permute-start | bytes 737288 | tf_op jit(solution)/shard_map/ppermute | solution.py:237
  201.1 8.1 %collective-permute-start.13 = (bf16[2,40,1536]{2,1,0:T(8,128)(2,1)S(1)}, bf16[2,40,1536]{2,1,0:T(8,128)(2,1)S(1)}, u32[]{:S(2)}, u32[]{:S(2)}) collective-permute-start(bf16[2,40,1536]{2,1,0:T(8,128)(2,1)S(1)} %slice.176), channel_id=1, source_target_pairs={{0,16},{16,0},{1,17},{17,1},{2,18},{18,2},{3,19},{19,3},{4,20},{20... | collective-permute-start | bytes 737288 | tf_op jit(solution)/shard_map/ppermute | solution.py:237
  207.6 4.9 %collective-permute-start.16 = (bf16[40,1536]{1,0:T(8,128)(2,1)S(1)}, bf16[40,1536]{1,0:T(8,128)(2,1)S(1)}, u32[]{:S(2)}, u32[]{:S(2)}) collective-permute-start(bf16[40,1536]{1,0:T(8,128)(2,1)S(1)} %dynamic-slice_bitcast_fusion.11), channel_id=1, source_target_pairs={{0,16},{16,0},{1,17},{17,1},{2,18},{18,2},{3,19},{19,3},{4,20},{20... | collective-permute-start | bytes 368648 | tf_op jit(solution)/shard_map/ppermute | solution.py:237
  210.6 8.1 %collective-permute-start.14 = (bf16[40,1536]{1,0:T(8,128)(2,1)}, bf16[40,1536]{1,0:T(8,128)(2,1)}, u32[]{:S(2)}, u32[]{:S(2)}) collective-permute-start(bf16[40,1536]{1,0:T(8,128)(2,1)} %dynamic-slice_bitcast_fusion.12), channel_id=1, source_target_pairs={{0,8},{4,12},{8,0},{12,4},{1,9},{5,13},{9,1},{13,5},{2,10},{6,14},... | collective-permute-start | bytes 368648 | tf_op jit(solution)/shard_map/ppermute | solution.py:237
  212.6 35.8 %all-to-all-start.3 = ((bf16[16,32,576]{2,1,0:T(8,128)(2,1)}), bf16[16,32,576]{2,1,0:T(8,128)(2,1)S(1)}, u32[]{:S(2)}, u32[]{:S(2)}) async-start(bf16[16,32,576]{2,1,0:T(8,128)(2,1)} %bitcast.239), calls=%async_computation.3 | async-start | bytes 1310720 | tf_op jit(solution)/shard_map/all_to_all | solution.py:255
  223.9 12.1 %collective-permute-start.19 = (bf16[80,384]{1,0:T(8,128)(2,1)S(1)}, bf16[80,384]{1,0:T(8,128)(2,1)S(1)}, u32[]{:S(2)}, u32[]{:S(2)}) collective-permute-start(bf16[80,384]{1,0:T(8,128)(2,1)S(1)} %bitcast.249), channel_id=1, source_target_pairs={{0,3},{1,2},{2,1},{3,0},{4,7},{5,6},{6,5},{7,4},{8,11},{9,10},{10,... | collective-permute-start | bytes 184328 | tf_op jit(solution)/shard_map/ppermute | solution.py:237
  227.8 14.1 %collective-permute-start.18 = (bf16[80,384]{1,0:T(8,128)(2,1)S(1)}, bf16[80,384]{1,0:T(8,128)(2,1)S(1)}, u32[]{:S(2)}, u32[]{:S(2)}) collective-permute-start(bf16[80,384]{1,0:T(8,128)(2,1)S(1)} %bitcast.250), channel_id=1, source_target_pairs={{0,2},{1,3},{2,0},{3,1},{4,6},{5,7},{6,4},{7,5},{8,10},{9,11},{10,... | collective-permute-start | bytes 184328 | tf_op jit(solution)/shard_map/ppermute | solution.py:237
  227.9 14.0 %collective-permute-start.17 = (bf16[80,384]{1,0:T(8,128)(2,1)S(1)}, bf16[80,384]{1,0:T(8,128)(2,1)S(1)}, u32[]{:S(2)}, u32[]{:S(2)}) collective-permute-start(bf16[80,384]{1,0:T(8,128)(2,1)S(1)} %bitcast.251), channel_id=1, source_target_pairs={{0,1},{1,0},{2,3},{3,2},{4,5},{5,4},{6,7},{7,6},{8,9},{9,8},{10,11... | collective-permute-start | bytes 184328 | tf_op jit(solution)/shard_map/ppermute | solution.py:237
  242.0 9.7 %collective-permute-start.20 = (bf16[80,384]{1,0:T(8,128)(2,1)S(1)}, bf16[80,384]{1,0:T(8,128)(2,1)}, u32[]{:S(2)}, u32[]{:S(2)}) collective-permute-start(bf16[80,384]{1,0:T(8,128)(2,1)S(1)} %fusion.21), channel_id=1, source_target_pairs={{0,1},{1,0},{2,3},{3,2},{4,5},{5,4},{6,7},{7,6},{8,9},{9,8},{10,11... | collective-permute-start | bytes 184328 | tf_op jit(solution)/shard_map/ppermute | solution.py:237
  242.0 10.5 %collective-permute-start.21 = (bf16[80,384]{1,0:T(8,128)(2,1)S(1)}, bf16[80,384]{1,0:T(8,128)(2,1)}, u32[]{:S(2)}, u32[]{:S(2)}) collective-permute-start(bf16[80,384]{1,0:T(8,128)(2,1)S(1)} %fusion.21), channel_id=1, source_target_pairs={{0,2},{1,3},{2,0},{3,1},{4,6},{5,7},{6,4},{7,5},{8,10},{9,11},{10,... | collective-permute-start | bytes 184328 | tf_op jit(solution)/shard_map/ppermute | solution.py:237
  243.9 9.6 %collective-permute-start.22 = (bf16[80,384]{1,0:T(8,128)(2,1)S(1)}, bf16[80,384]{1,0:T(8,128)(2,1)S(1)}, u32[]{:S(2)}, u32[]{:S(2)}) collective-permute-start(bf16[80,384]{1,0:T(8,128)(2,1)S(1)} %fusion.21), channel_id=1, source_target_pairs={{0,3},{1,2},{2,1},{3,0},{4,7},{5,6},{6,5},{7,4},{8,11},{9,10},{10,... | collective-permute-start | bytes 184328 | tf_op jit(solution)/shard_map/ppermute | solution.py:237
  259.4 7.9 %collective-permute-start.23 = (bf16[80,1536]{1,0:T(8,128)(2,1)S(1)}, bf16[80,1536]{1,0:T(8,128)(2,1)S(1)}, u32[]{:S(2)}, u32[]{:S(2)}) collective-permute-start(bf16[80,1536]{1,0:T(8,128)(2,1)S(1)} %bitcast.242), channel_id=1, source_target_pairs={{0,8},{4,12},{8,0},{12,4},{1,9},{5,13},{9,1},{13,5},{2,10},{6,14},... | collective-permute-start | bytes 737288 | tf_op jit(solution)/shard_map/ppermute | solution.py:237
  263.7 17.1 %collective-permute-start.28 = (bf16[2,112,1536]{2,1,0:T(8,128)(2,1)S(1)}, bf16[2,112,1536]{2,1,0:T(8,128)(2,1)S(1)}, u32[]{:S(2)}, u32[]{:S(2)}) collective-permute-start(bf16[2,112,1536]{2,1,0:T(8,128)(2,1)S(1)} %slice.188), channel_id=1, source_target_pairs={{0,8},{4,12},{8,0},{12,4},{1,9},{5,13},{9,1},{13,5},{2,10},{6,14},... | collective-permute-start | bytes 2064392 | tf_op jit(solution)/shard_map/ppermute | solution.py:237
  268.1 34.7 %collective-permute-start.24 = (bf16[2,80,1536]{2,1,0:T(8,128)(2,1)}, bf16[2,80,1536]{2,1,0:T(8,128)(2,1)}, u32[]{:S(2)}, u32[]{:S(2)}) collective-permute-start(bf16[2,80,1536]{2,1,0:T(8,128)(2,1)} %maximum_select_fusion.6), channel_id=1, source_target_pairs={{0,4},{4,0},{8,12},{12,8},{1,5},{5,1},{9,13},{13,9},{2,6},{6,2},{1... | collective-permute-start | bytes 1474568 | tf_op jit(solution)/shard_map/ppermute | solution.py:237
  268.4 18.4 %collective-permute-start.26 = (bf16[2,112,1536]{2,1,0:T(8,128)(2,1)S(1)}, bf16[2,112,1536]{2,1,0:T(8,128)(2,1)S(1)}, u32[]{:S(2)}, u32[]{:S(2)}) collective-permute-start(bf16[2,112,1536]{2,1,0:T(8,128)(2,1)S(1)} %slice.186), channel_id=1, source_target_pairs={{0,16},{16,0},{1,17},{17,1},{2,18},{18,2},{3,19},{19,3},{4,20},{20... | collective-permute-start | bytes 2064392 | tf_op jit(solution)/shard_map/ppermute | solution.py:237
  280.9 12.8 %collective-permute-start.29 = (bf16[112,1536]{1,0:T(8,128)(2,1)S(1)}, bf16[112,1536]{1,0:T(8,128)(2,1)S(1)}, u32[]{:S(2)}, u32[]{:S(2)}) collective-permute-start(bf16[112,1536]{1,0:T(8,128)(2,1)S(1)} %dynamic-slice_bitcast_fusion.8), channel_id=1, source_target_pairs={{0,16},{16,0},{1,17},{17,1},{2,18},{18,2},{3,19},{19,3},{4,20},{20... | collective-permute-start | bytes 1032200 | tf_op jit(solution)/shard_map/ppermute | solution.py:237
  287.0 9.9 %collective-permute-start.27 = (bf16[112,1536]{1,0:T(8,128)(2,1)S(1)}, bf16[112,1536]{1,0:T(8,128)(2,1)S(1)}, u32[]{:S(2)}, u32[]{:S(2)}) collective-permute-start(bf16[112,1536]{1,0:T(8,128)(2,1)S(1)} %dynamic-slice_bitcast_fusion.9), channel_id=1, source_target_pairs={{0,8},{4,12},{8,0},{12,4},{1,9},{5,13},{9,1},{13,5},{2,10},{6,14},... | collective-permute-start | bytes 1032200 | tf_op jit(solution)/shard_map/ppermute | solution.py:237
  298.2 9.1 %collective-permute-start.32 = (bf16[224,384]{1,0:T(8,128)(2,1)S(1)}, bf16[224,384]{1,0:T(8,128)(2,1)S(1)}, u32[]{:S(2)}, u32[]{:S(2)}) collective-permute-start(bf16[224,384]{1,0:T(8,128)(2,1)S(1)} %bitcast.245), channel_id=1, source_target_pairs={{0,3},{1,2},{2,1},{3,0},{4,7},{5,6},{6,5},{7,4},{8,11},{9,10},{10,... | collective-permute-start | bytes 516104 | tf_op jit(solution)/shard_map/ppermute | solution.py:237
  299.9 13.5 %collective-permute-start.31 = (bf16[224,384]{1,0:T(8,128)(2,1)S(1)}, bf16[224,384]{1,0:T(8,128)(2,1)S(1)}, u32[]{:S(2)}, u32[]{:S(2)}) collective-permute-start(bf16[224,384]{1,0:T(8,128)(2,1)S(1)} %bitcast.246), channel_id=1, source_target_pairs={{0,2},{1,3},{2,0},{3,1},{4,6},{5,7},{6,4},{7,5},{8,10},{9,11},{10,... | collective-permute-start | bytes 516104 | tf_op jit(solution)/shard_map/ppermute | solution.py:237
  300.0 13.4 %collective-permute-start.30 = (bf16[224,384]{1,0:T(8,128)(2,1)S(1)}, bf16[224,384]{1,0:T(8,128)(2,1)S(1)}, u32[]{:S(2)}, u32[]{:S(2)}) collective-permute-start(bf16[224,384]{1,0:T(8,128)(2,1)S(1)} %bitcast.247), channel_id=1, source_target_pairs={{0,1},{1,0},{2,3},{3,2},{4,5},{5,4},{6,7},{7,6},{8,9},{9,8},{10,11... | collective-permute-start | bytes 516104 | tf_op jit(solution)/shard_map/ppermute | solution.py:237
  313.5 5.5 %collective-permute-start.33 = (bf16[224,384]{1,0:T(8,128)(2,1)S(1)}, bf16[224,384]{1,0:T(8,128)(2,1)S(1)}, u32[]{:S(2)}, u32[]{:S(2)}) collective-permute-start(bf16[224,384]{1,0:T(8,128)(2,1)S(1)} %fusion.11), channel_id=1, source_target_pairs={{0,8},{4,12},{8,0},{12,4},{1,9},{5,13},{9,1},{13,5},{2,10},{6,14},... | collective-permute-start | bytes 516104 | tf_op jit(solution)/shard_map/ppermute | solution.py:237
  319.0 1.7 collective-permute-start.34
  (4 other events, 3.8 us)
